TPU v7x, 32 devices: a whole 2x2x4 slice. The times are simulated.
32 devices in a mesh: context: 16 (over z, x, core), tensor: 2 (over y).
Axes of the slice: x: 2, y: 2, z: 4, core: 2. Of those that a mesh axis runs over, the one named last changes fastest.
Arguments:
- head_inputs: bfloat16 [2048, 8192], P('context', 'tensor'), may hold values from -6 to 6
- step_sizes: float32 [128, 2048], P('tensor', 'context'), may hold values from 0.5 to 1.5
- decay_rate: float32 [128], P('tensor'), may hold values from 0.000146484375 to 0.05
- input_map: bfloat16 [2048, 1024], P('context', 'tensor'), may hold values from -0.5 to 0.5
- output_map: bfloat16 [2048, 1024], P('context', 'tensor'), may hold values from -0.5 to 0.5
- document: int32 [2048], P('context'), may hold values from 0 to 2, never falling along the last dimension, each value on 1 to 1024 neighbouring positions
- grad_output: bfloat16 [2048, 8192], P(('context', 'tensor')), may hold values from -6 to 6
Outputs:
- grad_inputs: bfloat16 [2048, 8192], P('context', 'tensor')
- grad_steps: float32 [128, 2048], P('tensor', 'context')
- grad_in_map: float32 [2048, 1024], P('context', 'tensor')
- grad_out_map: float32 [2048, 1024], P('context', 'tensor')
Inputs may be any that keep to these rules, and one draw needn't show every extreme that they name: document numbers never fall along the tokens; each document has 1 to 1024 tokens, one exactly 1024.
All inputs are finite; a program needn't handle non-finite values.
Results may differ from a plain program's by a relative error of at most 0.001.
Values may be sent and summed in bfloat16 or wider, within the bound.
A program may use at most 192 MiB of HBM per device.

v0:
```python
import jax
import jax.numpy as jnp
from jax import lax
from jax.sharding import PartitionSpec as P

H = 128
P_SIZE = 64
N = 128
G = 8
BLOCK = 128


HIGH = lax.Precision.HIGHEST


def padded(cells, sides, width):
    for axis, dim in sides:
        count = lax.axis_size(axis)
        ends = count - 1
        head = lax.slice_in_dim(cells, 0, width, axis=dim)
        tail = lax.slice_in_dim(cells, cells.shape[dim] - width, cells.shape[dim], axis=dim)
        cells = jnp.concatenate(
            [
                lax.ppermute(tail, axis, [(i, (i + 1) % count) for i in range(ends)]),
                cells,
                lax.ppermute(head, axis, [((i + 1) % count, i) for i in range(ends)]),
            ],
            axis=dim,
        )
    return cells


def entering(part, axis, combine, identity, reverse):
    count = lax.axis_size(axis)
    place = lax.axis_index(axis)
    ahead = count - 1 - place if reverse else place
    gathered = jax.tree.map(lambda a: lax.all_gather(a, axis), part)
    state = jax.tree.map(lambda a, e: jnp.zeros_like(a) + jnp.asarray(e, a.dtype), part, identity)

    def one(step, state):
        source = count - 1 - step if reverse else step
        return combine(
            state, jax.tree.map(lambda a: lax.dynamic_index_in_dim(a, source, 0, False), gathered)
        )

    return lax.fori_loop(0, ahead, one, state)


def link_pairs(earlier, later):
    decay_late = later[0]
    spread = decay_late.reshape(decay_late.shape + (1,) * (earlier[1].ndim - decay_late.ndim))
    return (earlier[0] * decay_late, spread * earlier[1] + later[1])


def shards(head_inputs, step_sizes, decay_rate, input_map, output_map, document, grad_output):
    heads_here = decay_rate.shape[0]
    tokens_here = head_inputs.shape[0]
    per_group = H // G
    groups_here = heads_here // per_group
    span = min(BLOCK, tokens_here)
    count = tokens_here // span
    local_grads = lax.all_to_all(grad_output, "tensor", split_axis=1, concat_axis=0, tiled=True)
    shifted_ids = document + 1
    rim = padded(shifted_ids, (("context", 0),), 1)
    prev_id = rim[0] - 1
    next_id = rim[-1] - 1
    ids_blocks = document.reshape(count, span)
    prev_blocks = jnp.concatenate([prev_id[None], ids_blocks[:-1, -1]])
    next_blocks = jnp.concatenate([ids_blocks[1:, 0], next_id[None]])
    positions = jnp.arange(span)
    lower = positions[:, None] >= positions[None, :]
    mask_blocks = (ids_blocks[:, :, None] == ids_blocks[:, None, :]) & lower[None]
    steps_heads = step_sizes.reshape(groups_here, per_group, count, span)
    rates = decay_rate.reshape(groups_here, per_group)
    cumul = jnp.cumsum(-rates[:, :, None, None] * steps_heads, axis=-1)
    step_rows = jnp.transpose(step_sizes).reshape(count, span, groups_here, per_group)
    inputs_f = head_inputs.astype(jnp.float32).reshape(count, span, groups_here, per_group, P_SIZE)
    scaled = inputs_f * step_rows[..., None]
    grads_f = local_grads.astype(jnp.float32).reshape(count, span, groups_here, per_group, P_SIZE)
    in_bf = input_map.reshape(count, span, groups_here, N)
    out_bf = output_map.reshape(count, span, groups_here, N)
    in_f = in_bf.astype(jnp.float32)
    out_f = out_bf.astype(jnp.float32)
    differ = cumul[..., :, None] - cumul[..., None, :]
    weights = jnp.where(
        mask_blocks[None, None], jnp.exp(jnp.where(mask_blocks[None, None], differ, 0.0)), 0.0
    )
    last_sum = cumul[..., -1:]
    in_coef = jnp.exp(cumul) * (ids_blocks == prev_blocks[:, None]).astype(jnp.float32)
    out_coef = jnp.exp(last_sum - cumul) * (ids_blocks == next_blocks[:, None]).astype(jnp.float32)
    end_coef = jnp.exp(last_sum - cumul) * (ids_blocks == ids_blocks[:, -1:]).astype(jnp.float32)
    block_link = (ids_blocks[:, -1] == prev_blocks).astype(jnp.float32)
    block_decay = jnp.exp(last_sum[..., 0]) * block_link
    fresh = jnp.einsum("kjgn,ghkj,kjghp->kghnp", in_f, end_coef, scaled, precision=HIGH)
    message = jnp.einsum("kign,ghki,kighp->kghnp", out_f, in_coef, grads_f, precision=HIGH)
    running = jnp.zeros_like(fresh[0])
    running_decay = jnp.ones_like(block_decay[..., 0])
    index = 0
    inner_states = running
    inner_decays = running_decay
    running = block_decay[..., index, None, None] * running + fresh[index]
    running_decay = block_decay[..., index] * running_decay
    later_states = [None] * count
    later_decays = [None] * count
    behind = jnp.zeros_like(message[0])
    behind_decay = jnp.ones_like(block_decay[..., 0])
    index = 0
    later_states[index] = behind
    later_decays[index] = behind_decay
    behind = block_decay[..., index, None, None] * behind + message[index]
    behind_decay = block_decay[..., index] * behind_decay
    _, incoming = entering(
        (running_decay, running),
        "context",
        link_pairs,
        (jnp.ones_like(running_decay), jnp.zeros_like(running)),
        False,
    )
    _, adjoint = entering(
        (behind_decay, behind),
        "context",
        link_pairs,
        (jnp.ones_like(behind_decay), jnp.zeros_like(behind)),
        True,
    )
    entry_states = jnp.stack([inner_decays[..., None, None] * incoming + inner_states], axis=0)
    exit_adjoints = jnp.stack(
        [later_decays[0][..., None, None] * adjoint + later_states[0]], axis=0
    )
    cross = jnp.einsum("kign,kjgn->gkij", out_bf, in_bf, preferred_element_type=jnp.float32)
    mixing = weights * cross[:, None]
    state_rows = jnp.einsum("kign,kghnp,ghki->kighp", out_f, entry_states, in_coef, precision=HIGH)
    adjoint_rows = jnp.einsum(
        "kjgn,kghnp,ghkj->kjghp", in_f, exit_adjoints, out_coef, precision=HIGH
    )
    carried_c = jnp.einsum("kighp,kghnp,ghki->kign", grads_f, entry_states, in_coef, precision=HIGH)
    carried_b = jnp.einsum(
        "kjghp,kghnp,ghkj->kjgn", scaled, exit_adjoints, out_coef, precision=HIGH
    )
    outputs = jnp.einsum("ghkij,kjghp->kighp", mixing, scaled, precision=HIGH) + state_rows
    update = jnp.einsum("ghkij,kighp->kjghp", mixing, grads_f, precision=HIGH) + adjoint_rows
    slope_rows = jnp.sum(grads_f * outputs, axis=-1) - jnp.sum(scaled * update, axis=-1)
    step_rows_part = jnp.sum(inputs_f * update, axis=-1)
    grad_inputs = (
        (update * step_rows[..., None])
        .reshape(tokens_here, heads_here * P_SIZE)
        .astype(jnp.bfloat16)
    )
    products = jnp.einsum("kighp,kjghp->ghkij", grads_f, scaled, precision=HIGH)
    score_grad = jnp.sum(weights * products, axis=1)
    grad_out_map = (
        jnp.einsum("gkij,kjgn->kign", score_grad, in_f, precision=HIGH) + carried_c
    ).reshape(tokens_here, groups_here * N)
    grad_in_map = (
        jnp.einsum("gkij,kign->kjgn", score_grad, out_f, precision=HIGH) + carried_b
    ).reshape(tokens_here, groups_here * N)
    slopes = jnp.transpose(slope_rows, (2, 3, 0, 1)).reshape(heads_here, tokens_here)
    step_terms = jnp.transpose(step_rows_part, (2, 3, 0, 1)).reshape(heads_here, tokens_here)
    token_index = jnp.arange(tokens_here)
    same_doc = (document[:, None] == document[None, :]) & (
        token_index[:, None] >= token_index[None, :]
    )
    tails_local = jnp.dot(
        slopes, same_doc.astype(jnp.float32), precision=HIGH, preferred_element_type=jnp.float32
    )
    tail_message = jnp.sum(slopes * (document == prev_id).astype(jnp.float32)[None, :], axis=1)
    linked = (document[-1] == prev_id).astype(jnp.float32)
    tail_link = linked * jnp.ones((heads_here,), jnp.float32)
    _, tail_carry = entering(
        (tail_link, tail_message),
        "context",
        link_pairs,
        (jnp.ones_like(tail_link), jnp.zeros_like(tail_message)),
        True,
    )
    tails = tails_local + tail_carry[:, None] * (document == next_id).astype(jnp.float32)[None, :]
    grad_steps = step_terms - decay_rate[:, None] * tails
    return (grad_inputs, grad_steps, grad_in_map, grad_out_map)


def solution(mesh):
    placed = (
        P("context", "tensor"),
        P("tensor", "context"),
        P("tensor"),
        P("context", "tensor"),
        P("context", "tensor"),
        P("context"),
        P(("context", "tensor"), None),
    )
    return jax.shard_map(
        shards,
        mesh=mesh,
        in_specs=placed,
        out_specs=(
            P("context", "tensor"),
            P("tensor", "context"),
            P("context", "tensor"),
            P("context", "tensor"),
        ),
        check_vma=False,
    )
```

profile of v0, /device:TPU:1, one launch (start us, length us, event | category | flops | bytes accessed | tf_op | source)
XLA Modules:
  0.0 581.3 jit_solution(4755453482523883967)
XLA Ops:
  8.5 4.5 collective-permute-start.1
  29.7 3.6 all-to-all-start
  34.2 11.9 %all-to-all-done = bf16[64,2,4096]{2,0,1:T(8,128)(2,1)S(1)} async-done(((bf16[64,2,4096]{2,0,1:T(8,128)(2,1)}), bf16[64,2,4096]{2,0,1:T(8,128)(2,1)S(1)}, u32[]{:S(2)}, u32[]{:S(2)}) %all-to-all-start) | async-done | bytes 1048608 | tf_op jit(solution)/shard_map/all_to_all | solution.py:62
  46.1 3.3 reshape.364
  49.4 4.1 copy.98
  53.5 3.8 fusion.14
  61.5 6.9 %fusion.2 = f32[4,16,64,128]{3,2,1,0:T(8,128)} fusion(f32[4,128,128]{1,2,0:T(8,128)S(1)} %fusion.62, f32[4,16,128]{2,1,0:T(8,128)} %bitcast.206, pred[128,128]{0,1:T(8,128)(4,1)S(1)} %fusion.55, f32[128,4,16,64]{0,3,2,1:T(8,128)S(1)} %bitcast.183, f32[128,4,16]{0,2,1:T(8,128)} %bitcast.198), kind=kOutput, calls=%fused_computation.12 | convolution fusion | flops 810024960 | bytes 4538368 | tf_op jit(solution)/shard_map/ghkij,kjghp->kighp/dot_general | solution.py:140
  71.6 31.6 %all-reduce = f32[16]{0:T(128)} all-reduce(f32[16]{0:T(128)} %dynamic-update-slice), channel_id=2, replica_groups=mesh['context'=16,'tensor'=2] {'context'}, use_global_device_ids=true, to_apply=%add | all-reduce | flops 16 | bytes 128
  103.2 22.3 %all-gather = f32[64,16,1,1]{1,3,2,0:T(1,128)} all-gather(f32[4,16,1,1]{1,3,2,0:T(1,128)} %bitcast.214), channel_id=3, replica_groups=mesh['context'=16,'tensor'=2] {'context'}, dimensions={0}, use_global_device_ids=true | all-gather | bytes 4352 | tf_op jit(solution)/shard_map/all_gather | solution.py:37
  127.0 4.6 reshape.373
  131.7 4.9 copy.112
  136.6 5.7 fusion
  144.4 6.2 %fusion.4 = f32[4,16,128,64]{2,3,1,0:T(8,128)} fusion(bf16[128,4,16,64]{0,3,2,1:T(8,128)(2,1)S(1)} %copy-done.2, f32[4,128,128]{1,2,0:T(8,128)S(1)} %copy-done.13, f32[4,16,128]{2,1,0:T(8,128)S(1)} %bitcast.208, pred[128,128]{0,1:T(8,128)(4,1)S(1)} %fusion.55), kind=kOutput, calls=%fused_computation.13 | convolution fusion | flops 809500672 | bytes 3457024 | tf_op jit(solution)/shard_map/ghkij,kighp->kjghp/dot_general | solution.py:141
  150.6 47.3 %all-gather.7.cloned.1.call-done = f32[16,4,16,128,64]{3,4,2,1,0:T(8,128)} async-done(((f32[1,4,16,128,64]{3,4,2,1,0:T(8,128)}), f32[16,4,16,128,64]{3,4,2,1,0:T(8,128)}) %all-gather.7.cloned.1.call-update) | async-done | bytes 33554448 | tf_op jit(solution)/shard_map/all_gather | solution.py:37
  200.4 12.4 %while.41 = (s32[]{:T(128)}, f32[4,16,128,64]{3,2,1,0:T(8,128)}, s32[]{:T(128)}, f32[16,4,16]{2,1,0:T(4,128)}, f32[16,4,16,128,64]{3,4,2,1,0:T(8,128)}, /*index=5*/s32[]{:T(128)}, s32[]{:T(128)}, s32[]{:T(128)}) while((s32[]{:T(128)}, f32[4,16,128,64]{3,2,1,0:T(8,128)}, s32[]{:T(128)}, f32[16,4,16]{2,1,0:T(4,128)}, ...), condition=%wide.region_5.6_spmd, body=%wide.region_4.5_spmd.sunk | while | flops 1048581 | bytes 14680959 | solution.py:46
  205.5 7.3 %bitcast_add_fusion.11 = f32[4,16,128,64]{3,2,1,0:T(8,128)} fusion(f32[1,4,16,128,64]{4,3,2,1,0:T(8,128)} %copy.165, f32[4,16,128,64]{3,2,1,0:T(8,128)} %get-tuple-element.452, f32[4,16]{1,0:T(4,128)S(1)} %dynamic-slice_bitcast_fusion.5), kind=kLoop, calls=%fused_computation.3.clone.1 | loop fusion | flops 1048576 | bytes 6291712 | tf_op jit(solution)/shard_map/while/body/add | solution.py:52
  212.8 7.0 %fusion.38 = f32[1,128,4,128]{1,3,2,0:T(8,128)} fusion(f32[1,128,4,128]{1,3,2,0:T(8,128)} %convolution_bitcast_fusion, f32[4,16,128,64]{3,2,1,0:T(8,128)} %get-tuple-element.217, bf16[128,4,16,64]{0,3,2,1:T(8,128)(2,1)S(1)} %copy-done.2, f32[4,16,128]{2,1,0:T(8,128)S(1)} %copy-done.9), kind=kOutput, calls=%fused_computation.55 | convolution fusion | flops 806420480 | bytes 3702784 | tf_op jit(solution)/shard_map/kighp,kghnp,ghki->kign/dot_general | solution.py:136
  221.7 7.0 %fusion.11 = f32[128,4,16]{0,2,1:T(8,128)} fusion(f32[1,128,4,16,64]{1,4,3,2,0:T(8,128)S(1)} %copy-done.3, f32[4,16,64,128]{3,2,1,0:T(8,128)} %fusion.2, f32[4,16,128,64]{3,2,1,0:T(8,128)} %get-tuple-element.217, f32[128,4,16]{0,2,1:T(8,128)S(1)} %bitcast.204, bf16[128,4,128,1]{2,1,0,3:T(4,128)(2,1)S(1)} %bitcast.193), kind=kOutput, calls=%fused_computation.21 | convolution fusion | flops 807395328 | bytes 6488064 | tf_op jit(solution)/shard_map/kign,kghnp,ghki->kighp/dot_general | solution.py:132
  228.7 139.3 %all-gather.5.cloned.1.call-done = f32[16,4,16,128,64]{3,4,2,1,0:T(8,128)} async-done(((f32[1,4,16,128,64]{3,4,2,1,0:T(8,128)}), f32[16,4,16,128,64]{3,4,2,1,0:T(8,128)}) %all-gather.5.cloned.1.call-update) | async-done | bytes 33554448 | tf_op jit(solution)/shard_map/all_gather | solution.py:37
  370.5 156.3 %while.40 = (s32[]{:T(128)}, f32[4,16,128,64]{3,2,1,0:T(8,128)}, s32[]{:T(128)}, f32[16,4,16]{2,1,0:T(4,128)}, f32[16,4,16,128,64]{3,4,2,1,0:T(8,128)}, /*index=5*/s32[]{:T(128)}, s32[]{:T(128)}, s32[]{:T(128)}, s32[]{:T(128)}) while((s32[]{:T(128)}, f32[4,16,128,64]{3,2,1,0:T(8,128)}, s32[]{:T(128)}, f32[16,4,16]{2,1,0:T(4,128)}, ...), condition=%wide.region_2.3_spmd, body=%wide.region_1.2_spmd.sunk | while | flops 1048582 | bytes 14680979 | solution.py:46
  375.7 6.0 %bitcast_add_fusion.10 = f32[4,16,128,64]{3,2,1,0:T(8,128)} fusion(f32[1,4,16,128,64]{4,3,2,1,0:T(8,128)} %copy.164, f32[4,16,128,64]{3,2,1,0:T(8,128)} %get-tuple-element.426, f32[4,16]{1,0:T(4,128)S(1)} %dynamic-slice_bitcast_fusion.4), kind=kLoop, calls=%fused_computation.clone.1 | loop fusion | flops 1048576 | bytes 6291712 | tf_op jit(solution)/shard_map/while/body/add | solution.py:52
  383.4 2.8 copy.164
  386.8 6.0 %bitcast_add_fusion.10 = f32[4,16,128,64]{3,2,1,0:T(8,128)} fusion(f32[1,4,16,128,64]{4,3,2,1,0:T(8,128)} %copy.164, f32[4,16,128,64]{3,2,1,0:T(8,128)} %get-tuple-element.426, f32[4,16]{1,0:T(4,128)S(1)} %dynamic-slice_bitcast_fusion.4), kind=kLoop, calls=%fused_computation.clone.1 | loop fusion | flops 1048576 | bytes 6291712 | tf_op jit(solution)/shard_map/while/body/add | solution.py:52
  394.6 2.8 copy.164
  398.0 6.0 %bitcast_add_fusion.10 = f32[4,16,128,64]{3,2,1,0:T(8,128)} fusion(f32[1,4,16,128,64]{4,3,2,1,0:T(8,128)} %copy.164, f32[4,16,128,64]{3,2,1,0:T(8,128)} %get-tuple-element.426, f32[4,16]{1,0:T(4,128)S(1)} %dynamic-slice_bitcast_fusion.4), kind=kLoop, calls=%fused_computation.clone.1 | loop fusion | flops 1048576 | bytes 6291712 | tf_op jit(solution)/shard_map/while/body/add | solution.py:52
  405.7 2.8 copy.164
  409.2 6.0 %bitcast_add_fusion.10 = f32[4,16,128,64]{3,2,1,0:T(8,128)} fusion(f32[1,4,16,128,64]{4,3,2,1,0:T(8,128)} %copy.164, f32[4,16,128,64]{3,2,1,0:T(8,128)} %get-tuple-element.426, f32[4,16]{1,0:T(4,128)S(1)} %dynamic-slice_bitcast_fusion.4), kind=kLoop, calls=%fused_computation.clone.1 | loop fusion | flops 1048576 | bytes 6291712 | tf_op jit(solution)/shard_map/while/body/add | solution.py:52
  416.9 2.8 copy.164
  420.3 6.0 %bitcast_add_fusion.10 = f32[4,16,128,64]{3,2,1,0:T(8,128)} fusion(f32[1,4,16,128,64]{4,3,2,1,0:T(8,128)} %copy.164, f32[4,16,128,64]{3,2,1,0:T(8,128)} %get-tuple-element.426, f32[4,16]{1,0:T(4,128)S(1)} %dynamic-slice_bitcast_fusion.4), kind=kLoop, calls=%fused_computation.clone.1 | loop fusion | flops 1048576 | bytes 6291712 | tf_op jit(solution)/shard_map/while/body/add | solution.py:52
  428.1 2.8 copy.164
  431.5 6.0 %bitcast_add_fusion.10 = f32[4,16,128,64]{3,2,1,0:T(8,128)} fusion(f32[1,4,16,128,64]{4,3,2,1,0:T(8,128)} %copy.164, f32[4,16,128,64]{3,2,1,0:T(8,128)} %get-tuple-element.426, f32[4,16]{1,0:T(4,128)S(1)} %dynamic-slice_bitcast_fusion.4), kind=kLoop, calls=%fused_computation.clone.1 | loop fusion | flops 1048576 | bytes 6291712 | tf_op jit(solution)/shard_map/while/body/add | solution.py:52
  439.2 2.8 copy.164
  442.7 6.0 %bitcast_add_fusion.10 = f32[4,16,128,64]{3,2,1,0:T(8,128)} fusion(f32[1,4,16,128,64]{4,3,2,1,0:T(8,128)} %copy.164, f32[4,16,128,64]{3,2,1,0:T(8,128)} %get-tuple-element.426, f32[4,16]{1,0:T(4,128)S(1)} %dynamic-slice_bitcast_fusion.4), kind=kLoop, calls=%fused_computation.clone.1 | loop fusion | flops 1048576 | bytes 6291712 | tf_op jit(solution)/shard_map/while/body/add | solution.py:52
  450.4 2.8 copy.164
  453.8 6.0 %bitcast_add_fusion.10 = f32[4,16,128,64]{3,2,1,0:T(8,128)} fusion(f32[1,4,16,128,64]{4,3,2,1,0:T(8,128)} %copy.164, f32[4,16,128,64]{3,2,1,0:T(8,128)} %get-tuple-element.426, f32[4,16]{1,0:T(4,128)S(1)} %dynamic-slice_bitcast_fusion.4), kind=kLoop, calls=%fused_computation.clone.1 | loop fusion | flops 1048576 | bytes 6291712 | tf_op jit(solution)/shard_map/while/body/add | solution.py:52
  461.6 2.8 copy.164
  465.0 6.0 %bitcast_add_fusion.10 = f32[4,16,128,64]{3,2,1,0:T(8,128)} fusion(f32[1,4,16,128,64]{4,3,2,1,0:T(8,128)} %copy.164, f32[4,16,128,64]{3,2,1,0:T(8,128)} %get-tuple-element.426, f32[4,16]{1,0:T(4,128)S(1)} %dynamic-slice_bitcast_fusion.4), kind=kLoop, calls=%fused_computation.clone.1 | loop fusion | flops 1048576 | bytes 6291712 | tf_op jit(solution)/shard_map/while/body/add | solution.py:52
  472.7 2.8 copy.164
  476.2 6.0 %bitcast_add_fusion.10 = f32[4,16,128,64]{3,2,1,0:T(8,128)} fusion(f32[1,4,16,128,64]{4,3,2,1,0:T(8,128)} %copy.164, f32[4,16,128,64]{3,2,1,0:T(8,128)} %get-tuple-element.426, f32[4,16]{1,0:T(4,128)S(1)} %dynamic-slice_bitcast_fusion.4), kind=kLoop, calls=%fused_computation.clone.1 | loop fusion | flops 1048576 | bytes 6291712 | tf_op jit(solution)/shard_map/while/body/add | solution.py:52
  483.9 2.8 copy.164
  487.3 6.0 %bitcast_add_fusion.10 = f32[4,16,128,64]{3,2,1,0:T(8,128)} fusion(f32[1,4,16,128,64]{4,3,2,1,0:T(8,128)} %copy.164, f32[4,16,128,64]{3,2,1,0:T(8,128)} %get-tuple-element.426, f32[4,16]{1,0:T(4,128)S(1)} %dynamic-slice_bitcast_fusion.4), kind=kLoop, calls=%fused_computation.clone.1 | loop fusion | flops 1048576 | bytes 6291712 | tf_op jit(solution)/shard_map/while/body/add | solution.py:52
  495.1 2.8 copy.164
  498.5 6.0 %bitcast_add_fusion.10 = f32[4,16,128,64]{3,2,1,0:T(8,128)} fusion(f32[1,4,16,128,64]{4,3,2,1,0:T(8,128)} %copy.164, f32[4,16,128,64]{3,2,1,0:T(8,128)} %get-tuple-element.426, f32[4,16]{1,0:T(4,128)S(1)} %dynamic-slice_bitcast_fusion.4), kind=kLoop, calls=%fused_computation.clone.1 | loop fusion | flops 1048576 | bytes 6291712 | tf_op jit(solution)/shard_map/while/body/add | solution.py:52
  509.7 6.0 %bitcast_add_fusion.10 = f32[4,16,128,64]{3,2,1,0:T(8,128)} fusion(f32[1,4,16,128,64]{4,3,2,1,0:T(8,128)} %copy.164, f32[4,16,128,64]{3,2,1,0:T(8,128)} %get-tuple-element.426, f32[4,16]{1,0:T(4,128)S(1)} %dynamic-slice_bitcast_fusion.4), kind=kLoop, calls=%fused_computation.clone.1 | loop fusion | flops 1048576 | bytes 6291712 | tf_op jit(solution)/shard_map/while/body/add | solution.py:52
  520.8 6.0 %bitcast_add_fusion.10 = f32[4,16,128,64]{3,2,1,0:T(8,128)} fusion(f32[1,4,16,128,64]{4,3,2,1,0:T(8,128)} %copy.164, f32[4,16,128,64]{3,2,1,0:T(8,128)} %get-tuple-element.426, f32[4,16]{1,0:T(4,128)S(1)} %dynamic-slice_bitcast_fusion.4), kind=kLoop, calls=%fused_computation.clone.1 | loop fusion | flops 1048576 | bytes 6291712 | tf_op jit(solution)/shard_map/while/body/add | solution.py:52
  526.9 7.7 %multiply_reduce_fusion = (f32[128,4,16]{0,2,1:T(8,128)S(1)}, f32[128,4,16]{0,2,1:T(8,128)}, bf16[1,128,4,16,64]{1,4,3,2,0:T(8,128)(2,1)S(1)}) fusion(f32[1,128,4,16,64]{1,4,3,2,0:T(8,128)} %bitcast.185, f32[128,4,16]{0,2,1:T(8,128)} %bitcast.200, f32[4,16,128,64]{3,2,1,0:T(8,128)} %get-tuple-element.216, bf16[128,4,128,1]{2,1,0,3:T(4,128)(2,1)S(1)} %bitcast.191, ...), kind=kOutput, calls=%fused_computation.31 | convolution fusion | flops 810008576 | bytes 7602176 | tf_op jit(solution)/shard_map/kjgn,kghnp,ghkj->kjghp/dot_general | solution.py:133
  534.7 28.2 %all-gather.1 = f32[16,1,64]{2,1,0:T(1,128)S(1)} all-gather(f32[1,1,64]{2,1,0:T(1,128)S(1)} %reshape.380), channel_id=1, replica_groups=mesh['context'=16,'tensor'=2] {'context'}, dimensions={0}, use_global_device_ids=true | all-gather | bytes 4352 | tf_op jit(solution)/shard_map/all_gather | solution.py:37
  563.7 6.7 %fusion.34 = f32[1,128,4,128]{1,3,2,0:T(8,128)} fusion(f32[1,128,4,128]{1,3,2,0:T(8,128)S(1)} %copy-done.6, f32[4,16,128,64]{3,2,1,0:T(8,128)} %get-tuple-element.216, f32[128,4,16,64]{0,3,2,1:T(8,128)S(1)} %bitcast.186, f32[4,16,128]{2,1,0:T(8,128)} %get-tuple-element.313, f32[128,4,16]{0,2,1:T(8,128)} %bitcast.201), kind=kOutput, calls=%fused_computation.53 | convolution fusion | flops 806420480 | bytes 4784128 | tf_op jit(solution)/shard_map/kjghp,kghnp,ghkj->kjgn/dot_general | solution.py:137
  (147 shorter events, 86.4 us)
Async XLA Ops:
  7.2 190.7 %all-gather.7.cloned.1.call-start = ((), (), s32[]{:S(2)}) async-start(), calls=%async_computation.2 | async-start | bytes 35651584 | tf_op jit(solution)/shard_map/all_gather | solution.py:37
  8.5 12.5 %collective-permute-start.1 = (s32[1]{0:T(128)}, s32[1]{0:T(128)}, u32[]{:S(2)}, u32[]{:S(2)}) collective-permute-start(s32[1]{0:T(128)} %get-tuple-element.319), channel_id=1, source_target_pairs={{0,2},{2,4},{4,6},{6,8},{8,10},{10,12},{12,14},{14,16},{16,18},{18... | collective-permute-start | bytes 20 | tf_op jit(solution)/shard_map/ppermute | solution.py:24
  13.0 9.9 %collective-permute-start = (s32[1]{0:T(128)}, s32[1]{0:T(128)}, u32[]{:S(2)}, u32[]{:S(2)}) collective-permute-start(s32[1]{0:T(128)} %get-tuple-element.318), channel_id=1, source_target_pairs={{2,0},{4,2},{6,4},{8,6},{10,8},{12,10},{14,12},{16,14},{18,16},{20... | collective-permute-start | bytes 20 | tf_op jit(solution)/shard_map/ppermute | solution.py:26
  18.8 5.3 copy-start.10
  19.0 1.8 copy-start.15
  20.7 2.8 copy-start.19
  20.7 4.1 copy-start.7
  20.9 115.7 %copy-start = (f32[128,4096]{0,1:T(8,128)}, f32[128,4096]{0,1:T(8,128)S(1)}, u32[]{:S(2)}) copy-start(f32[128,4096]{0,1:T(8,128)S(1)} %convert_element_type.47) | copy-start | bytes 6291460
  24.1 3.3 copy-start.17
  24.1 3.3 copy-start.21
  24.8 28.6 %copy-start.8 = (f32[4,16,128]{2,1,0:T(8,128)}, f32[4,16,128]{2,1,0:T(8,128)S(1)}, u32[]{:S(2)}) copy-start(f32[4,16,128]{2,1,0:T(8,128)S(1)} %get-tuple-element.314) | copy-start | bytes 98308
  27.4 1.2 copy-start.5
  29.7 16.4 %all-to-all-start = ((bf16[64,2,4096]{2,0,1:T(8,128)(2,1)}), bf16[64,2,4096]{2,0,1:T(8,128)(2,1)S(1)}, u32[]{:S(2)}, u32[]{:S(2)}) async-start(bf16[64,2,4096]{2,0,1:T(8,128)(2,1)} %bitcast.189), calls=%async_computation | async-start | bytes 2097152 | tf_op jit(solution)/shard_map/all_to_all | solution.py:62
  33.3 334.7 %all-gather.5.cloned.1.call-start = ((), (), s32[]{:S(2)}) async-start(), calls=%async_computation.1 | async-start | bytes 35651584 | tf_op jit(solution)/shard_map/all_gather | solution.py:37
  57.2 1.6 copy-start.25
  61.5 6.9 %copy-start.12 = (f32[4,128,128]{1,2,0:T(8,128)}, f32[4,128,128]{1,2,0:T(8,128)S(1)}, u32[]{:S(2)}) copy-start(f32[4,128,128]{1,2,0:T(8,128)S(1)} %fusion.62) | copy-start | bytes 786436
  131.7 4.9 copy-start.2
  136.6 5.7 copy-start.4
  136.6 7.8 %copy-start.11 = (f32[4,16,1,128]{3,1,2,0:T(8,128)S(1)}, f32[4,16,1,128]{3,1,2,0:T(8,128)}, u32[]{:S(2)}) copy-start(f32[4,16,1,128]{3,1,2,0:T(8,128)} %copy-done.10) | copy-start | bytes 98308
  136.6 7.8 %copy-start.13 = (f32[4,128,128]{1,2,0:T(8,128)S(1)}, f32[4,128,128]{1,2,0:T(8,128)}, u32[]{:S(2)}) copy-start(f32[4,128,128]{1,2,0:T(8,128)} %copy-done.12) | copy-start | bytes 786436
  200.4 12.4 %copy-start.9 = (f32[4,16,128]{2,1,0:T(8,128)S(1)}, f32[4,16,128]{2,1,0:T(8,128)}, u32[]{:S(2)}) copy-start(f32[4,16,128]{2,1,0:T(8,128)} %copy-done.8) | copy-start | bytes 98308
  212.8 8.9 %copy-start.3 = (f32[1,128,4,16,64]{1,4,3,2,0:T(8,128)S(1)}, f32[1,128,4,16,64]{1,4,3,2,0:T(8,128)}, u32[]{:S(2)}) copy-start(f32[1,128,4,16,64]{1,4,3,2,0:T(8,128)} %copy.112) | copy-start | bytes 6291460
  526.8 7.7 %copy-start.14 = (f32[128,4,16]{0,2,1:T(8,128)S(1)}, f32[128,4,16]{0,2,1:T(8,128)}, u32[]{:S(2)}) copy-start(f32[128,4,16]{0,2,1:T(8,128)} %fusion.11) | copy-start | bytes 98308
  526.8 7.7 %copy-start.18 = (f32[128]{0:T(128)S(1)}, f32[128]{0:T(128)}, u32[]{:S(2)}) copy-start(f32[128]{0:T(128)} %copy-done.17) | copy-start | bytes 1540
  526.8 36.1 %copy-start.23 = (f32[16]{0:T(128)S(1)}, f32[16]{0:T(128)}, u32[]{:S(2)}) copy-start(f32[16]{0:T(128)} %all-reduce) | copy-start | bytes 196
  526.9 36.8 %copy-start.1 = (f32[128,4096]{0,1:T(8,128)S(1)}, f32[128,4096]{0,1:T(8,128)}, u32[]{:S(2)}) copy-start(f32[128,4096]{0,1:T(8,128)} %copy-done) | copy-start | bytes 6291460
  526.9 36.8 %copy-start.6 = (f32[1,128,4,128]{1,3,2,0:T(8,128)S(1)}, f32[1,128,4,128]{1,3,2,0:T(8,128)}, u32[]{:S(2)}) copy-start(f32[1,128,4,128]{1,3,2,0:T(8,128)} %convolution_bitcast_fusion.1) | copy-start | bytes 786436
  570.4 3.1 copy-start.16
  570.4 3.1 copy-start.20
  570.4 3.1 copy-start.22
  570.4 3.1 copy-start.24
Sparse Core Ops, SparseCore 0:
  27.5 170.3 all-gather.6
  199.5 168.4 all-gather.4
where the time goes:
time: 583 us; the launch traced here: 581 us
  waiting for transfers between devices  199 us (34%)
  local copies, waits for them, and re-layouts  116 us (20%)
  other arithmetic  99.4 us (17%)
  blocking collectives  82.1 us (14%)
  matrix products  57.6 us (10%)
  between operations  16.9 us (3%)
  starting transfers between devices  10.1 us (2%)
    all_gather x2, waiting for transfers between devices, entering(): gathered = jax.tree.map(lambda a: lax.all_gather(a, axis), part)  187 us
    add x29, other arithmetic, link_pairs(): return (earlier[0] * decay_late, spread * earlier[1] + later[1])  91.6 us
    dynamic_slice x30, local copies, waits for them, and re-layouts, one(): lax.dynamic_index_in_dim(a, source, 0, False)  67.3 us
    all_gather x2, blocking collectives, entering(): gathered = jax.tree.map(lambda a: lax.all_gather(a, axis), part)  50.5 us
    unnamed x1, blocking collectives  31.6 us
    another operation x8, local copies, waits for them, and re-layouts  14.3 us
    all_to_all x1, waiting for transfers between devices, shards(): lax.all_to_all(grad_output, 'tensor', split_axis=1, concat_axis=0, tiled=...  11.9 us
  transfers between devices with their start and end apart: 5, of which 3 were waited for; matrix products, arithmetic and copies ran while one was open for 15% of the time, Pallas kernels for 0%

commit v1 on v0

v1 whole, which is shorter than its diff:
```python
import functools

import jax
import jax.numpy as jnp
from jax import lax
from jax.experimental import pallas as pl
from jax.experimental.pallas import tpu as pltpu
from jax.sharding import PartitionSpec as P

H = 128
P_SIZE = 64
N = 128
G = 8
SPAN = 128
PER = H // G
WIDE = PER * P_SIZE
LANES = 128
MESH = pl.DeviceIdType.MESH
BF = jnp.bfloat16
F32 = jnp.float32
NN = (((1,), (0,)), ((), ()))
NT = (((1,), (1,)), ((), ()))
TN = (((0,), (0,)), ((), ()))


def split(a):
    hi = a.astype(BF)
    return hi, (a - hi.astype(F32)).astype(BF)


def mm(a, b, dims=NN):
    return lax.dot_general(a, b, dims, preferred_element_type=F32)


def left2(a, b, dims=NN):
    hi, lo = split(a)
    return mm(hi, b, dims) + mm(lo, b, dims)


def right2(a, b, dims=NN):
    hi, lo = split(b)
    return mm(a, hi, dims) + mm(a, lo, dims)


def both3(a, b, dims=NN):
    ah, al = split(a)
    bh, bl = split(b)
    return mm(ah, bh, dims) + mm(ah, bl, dims) + mm(al, bh, dims)


def spreader():
    row = lax.broadcasted_iota(jnp.int32, (LANES, WIDE), 0)
    col = lax.broadcasted_iota(jnp.int32, (LANES, WIDE), 1)
    return jnp.where(row == col // P_SIZE, 1.0, 0.0).astype(BF)


def rows(k, size=SPAN):
    return pl.ds(k * size, size)


def ids_of(ranks):
    context = lax.axis_index("context")
    tensor = lax.axis_index("tensor")
    rank = lax.rem(context, ranks)
    return context - rank, rank, tensor


def greet(ranks, tensors, base, rank, tensor):
    barrier = pltpu.get_barrier_semaphore()
    for dr in range(ranks):
        for dt in range(tensors):
            if dr or dt:
                peer = {
                    "context": base + lax.rem(rank + dr, ranks),
                    "tensor": lax.rem(tensor + dt, tensors) if tensors > 1 else tensor,
                }
                pl.semaphore_signal(barrier, inc=1, device_id=peer, device_id_type=MESH)
    if ranks * tensors > 1:
        pl.semaphore_wait(barrier, ranks * tensors - 1)


def gather_kernel(ranks, tensors, x, b, c, dt, dy, xg, bg, cg, dtg, dyg, send, recv, local):
    base, rank, tensor = ids_of(ranks)
    greet(ranks, tensors, base, rank, tensor)
    part = dy.shape[0]
    spot = pl.multiple_of(rank * SPAN, SPAN)
    spot_dy = pl.multiple_of((rank * tensors + tensor) * part, part)
    copies = []
    order = [r for r in range(ranks) if r % 2 == 0] + [r for r in range(ranks) if r % 2]
    for dr in order[1:] + order[:1]:
        to = lax.rem(rank + dr, ranks)
        pairs = [
            (x.at[:, pl.ds(pl.multiple_of(to * WIDE, WIDE), WIDE)], xg.at[pl.ds(spot, SPAN), :]),
            (b.at[:, pl.ds(pl.multiple_of(to * N, N), N)], bg.at[pl.ds(spot, SPAN), :]),
            (c.at[:, pl.ds(pl.multiple_of(to * N, N), N)], cg.at[pl.ds(spot, SPAN), :]),
            (dt.at[pl.ds(pl.multiple_of(to * PER, PER), PER), :], dtg.at[rank]),
        ]
        for n, (src, dst) in enumerate(pairs):
            if dr == 0:
                copy = pltpu.make_async_copy(src, dst, local.at[n])
            else:
                copy = pltpu.make_async_remote_copy(
                    src_ref=src,
                    dst_ref=dst,
                    send_sem=send.at[dr * 4 + n],
                    recv_sem=recv.at[dr * 4 + n],
                    device_id={"context": base + to, "tensor": tensor},
                    device_id_type=MESH,
                )
            copy.start()
            copies.append(copy)
        for du in range(tensors):
            tt = lax.rem(tensor + du, tensors)
            at = pl.multiple_of((tt * ranks + to) * WIDE, WIDE)
            src, dst = dy.at[:, pl.ds(at, WIDE)], dyg.at[pl.ds(spot_dy, part), :]
            if dr == 0 and du == 0:
                copy = pltpu.make_async_copy(src, dst, local.at[4])
            else:
                n = ranks * 4 + dr * tensors + du
                copy = pltpu.make_async_remote_copy(
                    src_ref=src,
                    dst_ref=dst,
                    send_sem=send.at[n],
                    recv_sem=recv.at[n],
                    device_id={"context": base + to, "tensor": tt},
                    device_id_type=MESH,
                )
            copy.start()
            copies.append(copy)
    for copy in copies:
        copy.wait()


def scatter_kernel(ranks, gi, gs, gb, gc, gi_o, gs_o, gb_o, gc_o, send, recv, local):
    base, rank, tensor = ids_of(ranks)
    greet(ranks, 1, base, rank, tensor)
    wide_at = pl.multiple_of(rank * WIDE, WIDE)
    map_at = pl.multiple_of(rank * N, N)
    head_at = pl.multiple_of(rank * PER, PER)
    copies = []
    order = [r for r in range(ranks) if r % 2 == 0] + [r for r in range(ranks) if r % 2]
    for dr in order[1:] + order[:1]:
        to = lax.rem(rank + dr, ranks)
        spot = pl.multiple_of(to * SPAN, SPAN)
        pairs = [
            (gi.at[pl.ds(spot, SPAN), :], gi_o.at[:, pl.ds(wide_at, WIDE)]),
            (gb.at[pl.ds(spot, SPAN), :], gb_o.at[:, pl.ds(map_at, N)]),
            (gc.at[pl.ds(spot, SPAN), :], gc_o.at[:, pl.ds(map_at, N)]),
            (gs.at[to], gs_o.at[pl.ds(head_at, PER), :]),
        ]
        for n, (src, dst) in enumerate(pairs):
            if dr == 0:
                copy = pltpu.make_async_copy(src, dst, local.at[n])
            else:
                copy = pltpu.make_async_remote_copy(
                    src_ref=src,
                    dst_ref=dst,
                    send_sem=send.at[dr * 4 + n],
                    recv_sem=recv.at[dr * 4 + n],
                    device_id={"context": base + to, "tensor": tensor},
                    device_id_type=MESH,
                )
            copy.start()
            copies.append(copy)
    for copy in copies:
        copy.wait()


def summary_kernel(
    ranks, x, b, c, dt, dy, rate, tok, fresh, message, ltok, lhead, dttok, f_out, m_out, d_out
):
    spread = spreader()
    up = (
        lax.broadcasted_iota(jnp.int32, (SPAN, SPAN), 0)
        <= lax.broadcasted_iota(jnp.int32, (SPAN, SPAN), 1)
    ).astype(F32)
    pad = jnp.zeros((LANES - PER, SPAN), F32)
    decays = []
    for k in range(ranks):
        steps = dt[k]
        cum = lax.dot_general(
            -rate[...] * steps, up, NN, precision=lax.Precision.HIGHEST, preferred_element_type=F32
        )
        lhead[k] = cum
        cum_t = jnp.transpose(jnp.concatenate([cum, pad], axis=0))
        dt_t = jnp.transpose(jnp.concatenate([steps, pad], axis=0))
        ltok[rows(k), :] = cum_t
        dttok[rows(k), :] = dt_t
        mask_in = tok[rows(k), 1:2]
        mask_end = tok[rows(k), 3:4]
        in_coef = jnp.exp(cum_t) * mask_in
        end_coef = jnp.exp(cum_t[SPAN - 1 :, :] - cum_t) * mask_end * dt_t
        xs = x[rows(k), :].astype(F32) * left2(end_coef, spread)
        in_e = left2(in_coef, spread)
        dyc = dy[rows(k), :].astype(F32) * in_e
        fresh[k] = right2(b[rows(k), :], xs, TN)
        message[k] = right2(c[rows(k), :], dyc, TN)
        decays.append(in_e[SPAN - 1 :, :])
    total = fresh[0]
    decay = decays[0]
    for k in range(1, ranks):
        total = decays[k] * total + fresh[k]
        decay = decay * decays[k]
    f_out[...] = total
    d_out[...] = decay
    back = message[ranks - 1]
    for k in range(ranks - 2, -1, -1):
        back = decays[k] * back + message[k]
    m_out[...] = back


def local_kernel(x, b, c, dy, ltok, lhead, dttok, tok, idrow, u, agree, gb, gc):
    cross_t = mm(b[...], c[...], NT)
    later = lax.broadcasted_iota(jnp.int32, (SPAN, SPAN), 1) >= lax.broadcasted_iota(
        jnp.int32, (SPAN, SPAN), 0
    )
    same = tok[:, 0:1] == idrow[...]
    neg = jnp.where(later & same, 0.0, -1e30)
    score = jnp.zeros((SPAN, SPAN), F32)
    for h in range(PER):
        cut = slice(h * P_SIZE, (h + 1) * P_SIZE)
        x_h = x[:, cut]
        dy_h = dy[:, cut]
        w = jnp.exp((lhead[0, h : h + 1, :] - ltok[:, h : h + 1]) + neg)
        u[:, cut] = left2(w * cross_t, dy_h)
        q = w * mm(x_h, dy_h, NT) * dttok[:, h : h + 1]
        score = score + q
        agree[0, h : h + 1, :] = jnp.sum(q * cross_t, axis=0, keepdims=True)
    gb[...] = left2(score, c[...])
    gc[...] = left2(score, b[...], TN)


def finish_kernel(
    ranks, x, b, c, dy, rate, tok, idrow, ltok, dttok, u, agree, gb_l, gc_l, fresh, message,
    s_in, a_in, gi, gs, gb, gc, states,
):
    spread = spreader()
    states[0] = s_in[...]
    for k in range(ranks):
        last = ltok[k * SPAN + SPAN - 1 : k * SPAN + SPAN, :]
        link = tok[k * SPAN + SPAN - 1 : k * SPAN + SPAN, 1:2]
        decay = left2(jnp.broadcast_to(jnp.exp(last) * link, (8, LANES)), spread)[:1]
        states[k + 1] = decay * states[k] + fresh[k]
    pad = jnp.zeros((LANES - PER, SPAN), F32)
    earlier = lax.broadcasted_iota(jnp.int32, (SPAN, SPAN), 0) <= lax.broadcasted_iota(
        jnp.int32, (SPAN, SPAN), 1
    )
    rate_row = jnp.transpose(
        jnp.concatenate([jnp.broadcast_to(rate[...], (PER, SPAN)), pad], axis=0)
    )
    adj = a_in[...]
    for k in range(ranks - 1, -1, -1):
        at = rows(k)
        cum = ltok[at, :]
        dt_t = dttok[at, :]
        mask_in = tok[at, 1:2]
        mask_out = tok[at, 2:3]
        in_coef = jnp.exp(cum) * mask_in
        out_coef = jnp.exp(cum[SPAN - 1 :, :] - cum) * mask_out
        in_e = left2(in_coef, spread)
        out_e = left2(out_coef, spread)
        dt_e = left2(dt_t, spread)
        state = states[k]
        x_f = x[at, :].astype(F32)
        dyc = dy[at, :].astype(F32) * in_e
        total_u = u[at, :] + right2(b[at, :], adj) * out_e
        gi[at, :] = (total_u * dt_e).astype(BF)
        gc[at, :] = gc_l[at, :] + both3(dyc, state, NT)
        gb[at, :] = gb_l[at, :] + both3(x_f * out_e * dt_e, adj, NT)
        agree_t = jnp.transpose(jnp.concatenate([agree[k], pad], axis=0))
        dy_y = agree_t + left2(dyc * right2(c[at, :], state), spread, NT)
        xu = left2(x_f * total_u, spread, NT)
        slope = dy_y - dt_t * xu
        same = (tok[at, 0:1] == idrow[:, at]) & earlier
        meet = jnp.sum(states[k + 1] * adj, axis=0, keepdims=True)
        tail_carry = left2(jnp.broadcast_to(meet, (8, WIDE)), spread, NT)[:1]
        tails = right2(jnp.where(same, 1.0, 0.0).astype(BF), slope) + tail_carry * mask_out
        gs[k] = jnp.transpose(xu - rate_row * tails)[:PER, :]
        adj = in_e[SPAN - 1 :, :] * adj + message[k]


def shards(head_inputs, step_sizes, decay_rate, input_map, output_map, document, grad_output):
    heads_here = decay_rate.shape[0]
    ranks = heads_here // PER
    contexts = lax.axis_size("context")
    tensors = lax.axis_size("tensor")
    planes = contexts // ranks
    tokens = ranks * SPAN
    context = lax.axis_index("context")
    rank = context % ranks
    anywhere = pl.BlockSpec(memory_space=pl.ANY)
    vmem = pl.BlockSpec(memory_space=pltpu.VMEM)
    shape = jax.ShapeDtypeStruct

    ids = lax.all_gather(document, "context", tiled=True).astype(F32)
    blocks = ids.reshape(contexts, SPAN)
    none = jnp.full((1,), -1.0, F32)
    prev = jnp.concatenate([none, blocks[:-1, -1]])
    after = jnp.concatenate([blocks[1:, 0], none])
    marks = jnp.stack(
        [
            blocks,
            (blocks == prev[:, None]).astype(F32),
            (blocks == after[:, None]).astype(F32),
            (blocks == blocks[:, -1:]).astype(F32),
        ],
        axis=-1,
    ).reshape(contexts * SPAN, 4)
    start = (context - rank) * SPAN
    tok = lax.dynamic_slice(marks, (start, 0), (tokens, 4))
    idrow = lax.dynamic_slice(ids, (start,), (tokens,))[None, :]
    rate = lax.dynamic_slice(decay_rate, (rank * PER,), (PER,))[:, None]

    n_in = ranks * 4 + ranks * tensors
    xg, bg, cg, dtg, dyg = pl.pallas_call(
        functools.partial(gather_kernel, ranks, tensors),
        out_shape=(
            shape((tokens, WIDE), BF),
            shape((tokens, N), BF),
            shape((tokens, N), BF),
            shape((ranks, PER, SPAN), F32),
            shape((tokens, WIDE), BF),
        ),
        in_specs=[anywhere] * 5,
        out_specs=(anywhere,) * 5,
        scratch_shapes=[
            pltpu.SemaphoreType.DMA((n_in,)),
            pltpu.SemaphoreType.DMA((n_in,)),
            pltpu.SemaphoreType.DMA((5,)),
        ],
        compiler_params=pltpu.CompilerParams(collective_id=0, has_side_effects=True),
        name="spread_in",
    )(head_inputs, input_map, output_map, step_sizes, grad_output)

    state = shape((N, WIDE), F32)
    big = pltpu.CompilerParams(vmem_limit_bytes=48 * 1024 * 1024)
    fresh, message, ltok, lhead, dttok, f_out, m_out, d_out = pl.pallas_call(
        functools.partial(summary_kernel, ranks),
        out_shape=(
            shape((ranks, N, WIDE), F32),
            shape((ranks, N, WIDE), F32),
            shape((tokens, LANES), F32),
            shape((ranks, PER, SPAN), F32),
            shape((tokens, LANES), F32),
            state,
            state,
            shape((1, WIDE), F32),
        ),
        in_specs=[vmem] * 7,
        out_specs=(vmem,) * 8,
        compiler_params=big,
        name="summary",
    )(xg, bg, cg, dtg, dyg, rate, tok)

    def by_row(width):
        return pl.BlockSpec((SPAN, width), lambda k: (k, 0))

    per_block = pl.BlockSpec((1, PER, SPAN), lambda k: (k, 0, 0))
    u, agree, gb_l, gc_l = pl.pallas_call(
        local_kernel,
        grid=(ranks,),
        out_shape=(
            shape((tokens, WIDE), F32),
            shape((ranks, PER, SPAN), F32),
            shape((tokens, N), F32),
            shape((tokens, N), F32),
        ),
        in_specs=[
            by_row(WIDE),
            by_row(N),
            by_row(N),
            by_row(WIDE),
            by_row(LANES),
            per_block,
            by_row(LANES),
            by_row(4),
            pl.BlockSpec((1, SPAN), lambda k: (0, k)),
        ],
        out_specs=(by_row(WIDE), per_block, by_row(N), by_row(N)),
        compiler_params=big,
        cost_estimate=pl.CostEstimate(
            flops=8 * 10**9, bytes_accessed=8 * 10**6, transcendentals=10**6
        ),
        name="local",
    )(xg, bg, cg, dyg, ltok, lhead, dttok, tok, idrow)

    ahead = [(i, i + ranks) for i in range(contexts - ranks)]
    behind = [(i + ranks, i) for i in range(contexts - ranks)]
    s_move, a_move = f_out, m_out
    s_in = jnp.zeros_like(f_out)
    a_in = jnp.zeros_like(m_out)
    rounds = max(planes // 2, 1) if planes > 1 else 0
    for step in range(rounds):
        if step:
            s_move, a_move = d_out * s_move, d_out * a_move
        s_move = lax.ppermute(s_move, "context", ahead)
        a_move = lax.ppermute(a_move, "context", behind)
        s_in = s_in + s_move
        a_in = a_in + a_move

    gi, gs, gb, gc = pl.pallas_call(
        functools.partial(finish_kernel, ranks),
        out_shape=(
            shape((tokens, WIDE), BF),
            shape((ranks, PER, SPAN), F32),
            shape((tokens, N), F32),
            shape((tokens, N), F32),
        ),
        in_specs=[vmem] * 17,
        out_specs=(vmem,) * 4,
        scratch_shapes=[pltpu.VMEM((ranks + 1, N, WIDE), F32)],
        compiler_params=big,
        name="finish",
    )(
        xg, bg, cg, dyg, rate, tok, idrow, ltok, dttok, u, agree, gb_l, gc_l, fresh, message,
        s_in, a_in,
    )
    if ranks == 1:
        return gi, gs[0], gb, gc

    n_out = ranks * 4
    return pl.pallas_call(
        functools.partial(scatter_kernel, ranks),
        out_shape=(
            shape((SPAN, ranks * WIDE), BF),
            shape((heads_here, SPAN), F32),
            shape((SPAN, ranks * N), F32),
            shape((SPAN, ranks * N), F32),
        ),
        in_specs=[anywhere] * 4,
        out_specs=(anywhere,) * 4,
        scratch_shapes=[
            pltpu.SemaphoreType.DMA((n_out,)),
            pltpu.SemaphoreType.DMA((n_out,)),
            pltpu.SemaphoreType.DMA((4,)),
        ],
        compiler_params=pltpu.CompilerParams(collective_id=1, has_side_effects=True),
        name="spread_out",
    )(gi, gs, gb, gc)


def solution(mesh):
    placed = (
        P("context", "tensor"),
        P("tensor", "context"),
        P("tensor"),
        P("context", "tensor"),
        P("context", "tensor"),
        P("context"),
        P(("context", "tensor"), None),
    )
    return jax.shard_map(
        shards,
        mesh=mesh,
        in_specs=placed,
        out_specs=(
            P("context", "tensor"),
            P("tensor", "context"),
            P("context", "tensor"),
            P("context", "tensor"),
        ),
        check_vma=False,
    )
```

time: 583 us -> 139 us (0.24)
  waiting for transfers between devices: 199 us -> 16.3 us
  local copies, waits for them, and re-layouts: 116 us -> 14.5 us
  other arithmetic: 99.4 us -> 0.49 us
  Pallas kernels: 0 us -> 74.9 us
  blocking collectives: 82.1 us -> 23 us
  matrix products: 57.6 us -> 0 us
  between operations: 16.9 us -> 0.84 us
    all_gather x2 -> x0, waiting for transfers between devices: 187 us -> none  [entering(): gathered = jax.tree.map(lambda a: lax.all_gather(a, axis), part)]
    add x30 -> x2, other arithmetic: 92.2 us -> 0.11 us  [the longest x1 0.06 us: shards(): a_in = a_in + a_move]
    pallas_call x0 -> x5, Pallas kernels: none -> 74.9 us  [the longest x1 30 us: shards(): pl.pallas_call(functools.partial(gather_kernel, ranks, tensors), out_shap...]
    dynamic_slice x30 -> x1, local copies, waits for them, and re-layouts: 67.3 us -> 0.08 us  [shards(): idrow = lax.dynamic_slice(ids, (start,), (tokens,))[None, :]]
    dot_general x13 -> x0, matrix products: 57.6 us -> none  [the longest x1 7.68 us: shards(): jnp.einsum('kjgn,kghnp,ghkj->kjghp', in_f, exit_adjoints, out_coef, preci...]
    unnamed x1 -> x0, blocking collectives: 31.6 us -> none
    all_gather x2 -> x1, blocking collectives: 50.5 us -> 23 us  [shards(): ids = lax.all_gather(document, 'context', tiled=True).astype(F32)]
    ppermute x2 -> x4, waiting for transfers between devices: 0.01 us -> 16.3 us  [the longest x2 10.8 us: shards(): s_move = lax.ppermute(s_move, 'context', ahead)]
  transfers between devices with their start and end apart: 5 -> 4, of which waited for: 3 -> 4; matrix products, arithmetic and copies ran while one was open for 15% -> 0% of each run, Pallas kernels for 0% -> 4%
where the time goes in v1:
time: 139 us; the launch traced here: 138 us
  Pallas kernels  74.9 us (54%)
  blocking collectives  23 us (17%)
  waiting for transfers between devices  16.3 us (12%)
  local copies, waits for them, and re-layouts  14.5 us (10%)
  starting transfers between devices  8.09 us (6%)
    pallas_call x1, Pallas kernels, shards(): pl.pallas_call(functools.partial(gather_kernel, ranks, tensors), out_shap...  30 us
    all_gather x1, blocking collectives, shards(): ids = lax.all_gather(document, 'context', tiled=True).astype(F32)  23 us
    pallas_call x1, Pallas kernels, shards(): pl.pallas_call(functools.partial(scatter_kernel, ranks), out_shape=(shape...  22.4 us
    unnamed x35, local copies, waits for them, and re-layouts  13.9 us
    pallas_call x1, Pallas kernels, shards(): pl.pallas_call(functools.partial(finish_kernel, ranks), out_shape=(shape(...  11.1 us
    ppermute x2, waiting for transfers between devices, shards(): s_move = lax.ppermute(s_move, 'context', ahead)  10.8 us
    pallas_call x1, Pallas kernels, shards(): pl.pallas_call(local_kernel, grid=(ranks,), out_shape=(shape((tokens, WID...  5.74 us
    pallas_call x1, Pallas kernels, shards(): pl.pallas_call(functools.partial(summary_kernel, ranks), out_shape=(shape...  5.66 us
  transfers between devices with their start and end apart: 4, of which 4 were waited for; matrix products, arithmetic and copies ran while one was open for 0% of the time, Pallas kernels for 4%

profile of v1, /device:TPU:1, one launch (start us, length us, event | category | flops | bytes accessed | tf_op | source)
XLA Modules:
  0.0 138.2 jit_solution(13064190469626225649)
XLA Ops:
  0.6 0.0 copy-start
  0.7 23.0 %all-gather = s32[16,1,128]{2,1,0:T(1,128)S(1)} all-gather(s32[1,1,128]{2,1,0:T(1,128)} %bitcast.39), channel_id=1, replica_groups=mesh['context'=16,'tensor'=2] {'context'}, dimensions={0}, use_global_device_ids=true | all-gather | bytes 8704 | tf_op jit(solution)/shard_map/all_gather | solution.py:295
  23.6 0.2 slice_reduce_fusion
  23.8 0.2 slice_reduce_fusion.1
  24.0 0.0 copy-done
  24.0 0.1 dynamic-slice_bitcast_fusion
  24.1 0.1 copy.22.rate
  24.2 0.1 pad_maximum_fusion
  24.3 0.1 fusion.5
  24.4 0.1 fusion.2
  24.5 0.1 copy.23.tok
  24.6 30.0 %spread_in.1 = (bf16[512,1024]{1,0:T(8,128)(2,1)}, bf16[512,128]{1,0:T(8,128)(2,1)}, bf16[512,128]{1,0:T(8,128)(2,1)}, f32[4,16,128]{2,1,0:T(8,128)}, bf16[512,1024]{1,0:T(8,128)(2,1)}) custom-call(bf16[128,4096]{1,0:T(8,128)(2,1)} %x.1, bf16[128,512]{1,0:T(8,128)(2,1)} %b.1, bf16[128,512]{1,0:T(8,128)(2,1)} %c.1, f32[64,128]{1,0:T(8,128)} %dt.1, ...), custom_call_target="tpu_custom_call" | custom-call | tf_op jit(solution)/shard_map/spread_in/pallas_call | solution.py:315
  54.6 0.0 copy-start.1
  54.6 1.2 copy-done.1
  55.9 1.2 copy-done.2
  57.1 0.9 copy-done.6
  58.0 0.9 copy-done.7
  58.9 0.8 copy-done.11
  59.6 5.7 %summary.1 = (f32[4,128,1024]{2,1,0:T(8,128)}, f32[4,128,1024]{2,1,0:T(8,128)}, f32[512,128]{1,0:T(8,128)S(1)}, f32[4,16,128]{2,1,0:T(8,128)S(1)}, f32[512,128]{...) custom-call(bf16[512,1024]{1,0:T(8,128)(2,1)S(1)} %copy-done.1, ...), custom_call_target="tpu_custom_call" | custom-call | tf_op jit(solution)/shard_map/summary/pallas_call | solution.py:337
  65.3 1.3 collective-permute-start
  66.6 1.3 collective-permute-start.2
  67.9 0.1 dynamic_slice.11
  68.0 10.0 %collective-permute-done = f32[128,1024]{1,0:T(8,128)S(1)} collective-permute-done((f32[128,1024]{1,0:T(8,128)S(1)}, f32[128,1024]{1,0:T(8,128)S(1)}, u32[]{:S(2)}, u32[]{:S(2)}) %collective-permute-start) | collective-permute-done | bytes 524320 | tf_op jit(solution)/shard_map/ppermute | solution.py:396
  78.0 3.8 %collective-permute-done.2 = f32[128,1024]{1,0:T(8,128)S(1)} collective-permute-done((f32[128,1024]{1,0:T(8,128)S(1)}, f32[128,1024]{1,0:T(8,128)S(1)}, u32[]{:S(2)}, u32[]{:S(2)}) %collective-permute-start.2) | collective-permute-done | bytes 524320 | tf_op jit(solution)/shard_map/ppermute | solution.py:397
  81.8 0.1 broadcast_multiply_fusion
  82.0 1.3 collective-permute-start.3
  83.3 4.2 %collective-permute-start.1 = (f32[128,1024]{1,0:T(8,128)S(1)}, f32[128,1024]{1,0:T(8,128)S(1)}, u32[]{:S(2)}, u32[]{:S(2)}) collective-permute-start(f32[128,1024]{1,0:T(8,128)S(1)} %get-tuple-element.54), channel_id=1, source_target_pairs={{0,8},{2,10},{4,12},{6,14},{8,16},{10,18},{12,20},{14,22},{16,24},... | collective-permute-start | bytes 1572872 | tf_op jit(solution)/shard_map/ppermute | solution.py:396
  87.5 0.0 copy-done.3
  87.5 5.7 %local.1 = (f32[512,1024]{1,0:T(8,128)S(1)}, f32[4,16,128]{2,1,0:T(8,128)S(1)}, f32[512,128]{1,0:T(8,128)S(1)}, f32[512,128]{1,0:T(8,128)S(1)}) custom-call(bf16[512,1024]{1,0:T(8,128)(2,1)S(1)} %copy-done.1, bf16[512,128]{1,0:T(8,128)(2,1)S(1)} %copy-done.6, bf16[512,128]{1,0:T(8,128)(2,1)S(1)} %copy-done.7, bf16[512,1024]{1,0:T(8,128)(2,1)S(1)} %copy-done.3, ...), custom_call_target="tpu_custom_call" | custom-call | flops 8000000000 | bytes 8000000 | tf_op jit(solution)/shard_map/local/pallas_call | solution.py:359
  93.2 0.0 copy-start.4
  93.3 1.3 copy-done.4
  94.6 1.7 %collective-permute-done.3 = f32[128,1024]{1,0:T(8,128)S(1)} collective-permute-done((f32[128,1024]{1,0:T(8,128)S(1)}, f32[128,1024]{1,0:T(8,128)S(1)}, u32[]{:S(2)}, u32[]{:S(2)}) %collective-permute-start.3) | collective-permute-done | bytes 524320 | tf_op jit(solution)/shard_map/ppermute | solution.py:397
  96.3 0.1 add.21.a_in
  96.3 0.8 collective-permute-done.1
  97.2 0.1 add.20.s_in
  97.2 11.1 %finish.1 = (bf16[512,1024]{1,0:T(8,128)(2,1)S(1)}, f32[4,16,128]{2,1,0:T(8,128)S(1)}, f32[512,128]{1,0:T(8,128)S(1)}, f32[512,128]{1,0:T(8,128)S(1)}) custom-call(bf16[512,1024]{1,0:T(8,128)(2,1)S(1)} %copy-done.1, bf16[512,128]{1,0:T(8,128)(2,1)S(1)} %copy-done.6, bf16[512,128]{1,0:T(8,128)(2,1)S(1)} %copy-done.7, bf16[512,1024]{1,0:T(8,128)(2,1)} %get-tuple-element.28.dy, ...), custom_call_target="tpu_custom_call" | custom-call | tf_op jit(solution)/shard_map/finish/pallas_call | solution.py:401
  108.3 1.0 copy-done.5
  109.3 0.7 copy-done.8
  110.0 0.7 copy-done.9
  110.7 0.6 copy-done.10
  111.3 22.4 %spread_out.1 = (bf16[128,4096]{1,0:T(8,128)(2,1)}, f32[64,128]{1,0:T(8,128)}, f32[128,512]{1,0:T(8,128)}, f32[128,512]{1,0:T(8,128)}) custom-call(bf16[512,1024]{1,0:T(8,128)(2,1)} %copy-done.5, f32[4,16,128]{2,1,0:T(8,128)} %copy-done.10, f32[512,128]{1,0:T(8,128)} %copy-done.8, f32[512,128]{1,0:T(8,128)} %copy-done.9), custom_call_target="tpu_custom_call" | custom-call | tf_op jit(solution)/shard_map/spread_out/pallas_call | solution.py:422
  133.8 0.0 copy-start.14
  133.8 0.0 copy-start.13
  133.8 2.3 %copy.28 = bf16[128,4096]{1,0:T(8,128)(2,1)} copy(bf16[128,4096]{1,0:T(8,128)(2,1)} %get-tuple-element.61) | data formatting | bytes 2097152
  136.1 0.6 copy.29
  136.8 0.0 copy-done.13
  136.8 0.7 copy.30
  137.5 0.7 copy.31
  (14 shorter events, 0.0 us)
Async XLA Ops:
  0.6 23.4 %copy-start = (f32[64]{0:T(128)S(1)}, f32[64]{0:T(128)}, u32[]{:S(2)}) copy-start(f32[64]{0:T(128)} %param.9) | copy-start | bytes 772
  54.6 1.2 copy-start.1
  55.9 1.2 copy-start.2
  57.1 0.9 copy-start.6
  58.0 0.9 copy-start.7
  58.9 0.8 copy-start.11
  59.6 27.8 %copy-start.3 = (bf16[512,1024]{1,0:T(8,128)(2,1)S(1)}, bf16[512,1024]{1,0:T(8,128)(2,1)}, u32[]{:S(2)}) copy-start(bf16[512,1024]{1,0:T(8,128)(2,1)} %get-tuple-element.28.dy) | copy-start | bytes 3145732
  65.3 12.7 %collective-permute-start = (f32[128,1024]{1,0:T(8,128)S(1)}, f32[128,1024]{1,0:T(8,128)S(1)}, u32[]{:S(2)}, u32[]{:S(2)}) collective-permute-start(f32[128,1024]{1,0:T(8,128)S(1)} %get-tuple-element.39), channel_id=1, source_target_pairs={{0,8},{2,10},{4,12},{6,14},{8,16},{10,18},{12,20},{14,22},{16,24},... | collective-permute-start | bytes 1572872 | tf_op jit(solution)/shard_map/ppermute | solution.py:396
  66.6 15.2 %collective-permute-start.2 = (f32[128,1024]{1,0:T(8,128)S(1)}, f32[128,1024]{1,0:T(8,128)S(1)}, u32[]{:S(2)}, u32[]{:S(2)}) collective-permute-start(f32[128,1024]{1,0:T(8,128)S(1)} %get-tuple-element.41), channel_id=1, source_target_pairs={{8,0},{10,2},{12,4},{14,6},{16,8},{18,10},{20,12},{22,14},{24,16},... | collective-permute-start | bytes 1572872 | tf_op jit(solution)/shard_map/ppermute | solution.py:397
  82.0 14.3 %collective-permute-start.3 = (f32[128,1024]{1,0:T(8,128)S(1)}, f32[128,1024]{1,0:T(8,128)S(1)}, u32[]{:S(2)}, u32[]{:S(2)}) collective-permute-start(f32[128,1024]{1,0:T(8,128)S(1)} %get-tuple-element.53), channel_id=1, source_target_pairs={{8,0},{10,2},{12,4},{14,6},{16,8},{18,10},{20,12},{22,14},{24,16},... | collective-permute-start | bytes 1572872 | tf_op jit(solution)/shard_map/ppermute | solution.py:397
  83.3 13.9 %collective-permute-start.1 = (f32[128,1024]{1,0:T(8,128)S(1)}, f32[128,1024]{1,0:T(8,128)S(1)}, u32[]{:S(2)}, u32[]{:S(2)}) collective-permute-start(f32[128,1024]{1,0:T(8,128)S(1)} %get-tuple-element.54), channel_id=1, source_target_pairs={{0,8},{2,10},{4,12},{6,14},{8,16},{10,18},{12,20},{14,22},{16,24},... | collective-permute-start | bytes 1572872 | tf_op jit(solution)/shard_map/ppermute | solution.py:396
  93.2 1.4 copy-start.4
  108.3 1.0 copy-start.5
  109.3 0.7 copy-start.8
  110.0 0.7 copy-start.9
  110.7 0.6 copy-start.10
  133.8 2.4 %copy-start.14 = (f32[64,128]{1,0:T(8,128)S(1)}, f32[64,128]{1,0:T(8,128)}, u32[]{:S(2)}) copy-start(f32[64,128]{1,0:T(8,128)} %get-tuple-element.62) | copy-start | bytes 98308
  133.8 3.0 %copy-start.13 = (f32[128,512]{1,0:T(8,128)S(1)}, f32[128,512]{1,0:T(8,128)}, u32[]{:S(2)}) copy-start(f32[128,512]{1,0:T(8,128)} %get-tuple-element.63) | copy-start | bytes 786436
  133.8 3.7 %copy-start.12 = (f32[128,512]{1,0:T(8,128)S(1)}, f32[128,512]{1,0:T(8,128)}, u32[]{:S(2)}) copy-start(f32[128,512]{1,0:T(8,128)} %get-tuple-element.64) | copy-start | bytes 786436

commit v2 on v0

v2 whole, which is shorter than its diff:
```python
import functools

import jax
import jax.numpy as jnp
from jax import lax
from jax.experimental import pallas as pl
from jax.experimental.pallas import tpu as pltpu
from jax.sharding import PartitionSpec as P

H = 128
P_SIZE = 64
N = 128
G = 8
SPAN = 128
PER = H // G
WIDE = PER * P_SIZE
LANES = 128
CHUNKS = 4
HC = PER // CHUNKS
CW = HC * P_SIZE
MESH = pl.DeviceIdType.MESH
BF = jnp.bfloat16
F32 = jnp.float32
NN = (((1,), (0,)), ((), ()))
NT = (((1,), (1,)), ((), ()))
TN = (((0,), (0,)), ((), ()))


def split(a):
    hi = a.astype(BF)
    return hi, (a - hi.astype(F32)).astype(BF)


def mm(a, b, dims=NN):
    return lax.dot_general(a, b, dims, preferred_element_type=F32)


def left2(a, b, dims=NN):
    hi, lo = split(a)
    return mm(hi, b, dims) + mm(lo, b, dims)


def right2(a, b, dims=NN):
    hi, lo = split(b)
    return mm(a, hi, dims) + mm(a, lo, dims)


def both3(a, b, dims=NN):
    ah, al = split(a)
    bh, bl = split(b)
    return mm(ah, bh, dims) + mm(ah, bl, dims) + mm(al, bh, dims)


def rows(k, size=SPAN):
    return pl.ds(k * size, size)


def mega_kernel(
    ranks, tensors, contexts, x, b, c, dt, dy, doc, rate, gi_o, gs_o, gb_o, gc_o,
    xg, dyg, bg, cg, dtg, docs, s_in, a_in, s_out, a_out, fresh, message, u, gi,
    tc, ltok, dttok, c_in, c_out, c_end, idcol, lhead, cross, neg, score, agree,
    dyy, xu, meets, gb, gc, gs,
    send_x, recv_x, send_dy, recv_dy, send_s, recv_s, send_doc, recv_doc,
    send_z, recv_z, send_o, recv_o, send_m, recv_m, local,
):
    planes = contexts // ranks
    last = planes - 1
    context = lax.axis_index("context")
    tensor = lax.axis_index("tensor")
    rank = lax.rem(context, ranks)
    base = context - rank
    plane = lax.div(context, ranks)
    part = dy.shape[0]
    spot = pl.multiple_of(rank * SPAN, SPAN)
    spot_dy = pl.multiple_of((rank * tensors + tensor) * part, part)

    barrier = pltpu.get_barrier_semaphore()
    for d in range(1, contexts):
        pl.semaphore_signal(
            barrier, inc=1,
            device_id={"context": lax.rem(context + d, contexts), "tensor": tensor},
            device_id_type=MESH,
        )
    for dr in range(ranks):
        for du in range(1, tensors):
            pl.semaphore_signal(
                barrier, inc=1,
                device_id={
                    "context": base + lax.rem(rank + dr, ranks),
                    "tensor": lax.rem(tensor + du, tensors),
                },
                device_id_type=MESH,
            )
    pl.semaphore_wait(barrier, contexts - 1 + ranks * (tensors - 1))

    def remote(src, dst, send, recv, ctx, ten):
        return pltpu.make_async_remote_copy(
            src_ref=src, dst_ref=dst, send_sem=send, recv_sem=recv,
            device_id={"context": ctx, "tensor": ten}, device_id_type=MESH,
        )

    def doc_copy(d):
        to = lax.rem(context + d, contexts)
        return remote(doc, docs.at[context], send_doc.at[d], recv_doc.at[d], to, tensor)

    def small_copies(dr):
        to = lax.rem(rank + dr, ranks)
        at = pl.multiple_of(to * N, N)
        pairs = [
            (dt.at[pl.ds(pl.multiple_of(to * PER, PER), PER), :], dtg.at[rank]),
            (b.at[:, pl.ds(at, N)], bg.at[pl.ds(spot, SPAN), :]),
            (c.at[:, pl.ds(at, N)], cg.at[pl.ds(spot, SPAN), :]),
        ]
        if dr == 0:
            return [pltpu.make_async_copy(s, d, local.at[n]) for n, (s, d) in enumerate(pairs)]
        return [
            remote(s, d, send_s.at[dr * 3 + n], recv_s.at[dr * 3 + n], base + to, tensor)
            for n, (s, d) in enumerate(pairs)
        ]

    def chunk_copies(ch):
        copies = []
        for dr in list(range(1, ranks)) + [0]:
            to = lax.rem(rank + dr, ranks)
            src = x.at[:, pl.ds(pl.multiple_of(to * WIDE + ch * CW, CW), CW)]
            dst = xg.at[ch, pl.ds(spot, SPAN), :]
            if dr == 0:
                copies.append(pltpu.make_async_copy(src, dst, recv_x.at[ch, 0]))
            else:
                copies.append(
                    remote(src, dst, send_x.at[ch, dr], recv_x.at[ch, dr], base + to, tensor)
                )
            for du in range(tensors):
                tt = lax.rem(tensor + du, tensors)
                at = pl.multiple_of((tt * ranks + to) * WIDE + ch * CW, CW)
                src, dst = dy.at[:, pl.ds(at, CW)], dyg.at[ch, pl.ds(spot_dy, part), :]
                n = dr * tensors + du
                if n == 0:
                    copies.append(pltpu.make_async_copy(src, dst, recv_dy.at[ch, 0]))
                else:
                    copies.append(
                        remote(src, dst, send_dy.at[ch, n], recv_dy.at[ch, n], base + to, tt)
                    )
        return copies

    def wait_in(copy):
        if copy.is_remote:
            copy.wait_recv()
        else:
            copy.wait()

    own_doc = pltpu.make_async_copy(doc, docs.at[context], local.at[3])
    own_doc.start()
    for dr in list(range(1, ranks)) + [0]:
        for copy in small_copies(dr):
            copy.start()
    for d in range(1, contexts):
        doc_copy(d).start()
    for ch in range(CHUNKS):
        for copy in chunk_copies(ch):
            copy.start()

    @pl.when(plane == 0)
    def _():
        s_in[...] = jnp.zeros_like(s_in)

    @pl.when(plane == last)
    def _():
        a_in[...] = jnp.zeros_like(a_in)

    score[...] = jnp.zeros_like(score)
    dyy[...] = jnp.zeros_like(dyy)
    xu[...] = jnp.zeros_like(xu)
    meets[...] = jnp.zeros_like(meets)
    gb[...] = jnp.zeros_like(gb)
    gc[...] = jnp.zeros_like(gc)

    row_i = lax.broadcasted_iota(jnp.int32, (SPAN, SPAN), 0)
    col_i = lax.broadcasted_iota(jnp.int32, (SPAN, SPAN), 1)
    ordered = row_i <= col_i
    up = ordered.astype(F32)
    pad = jnp.zeros((LANES - PER, SPAN), F32)

    own_doc.wait()
    for d in range(1, contexts):
        doc_copy(d).wait_recv()
    for dr in list(range(1, ranks)) + [0]:
        for copy in small_copies(dr):
            wait_in(copy)
    before = docs[jnp.maximum(base - 1, 0)][:, SPAN - 1 :]
    before = jnp.where(plane == 0, -1.0, before)
    after = docs[jnp.minimum(base + ranks, contexts - 1)][:, :1]
    after = jnp.where(plane == last, -1.0, after)
    id_rows = [docs[base + k] for k in range(ranks)]
    for k in range(ranks):
        at = rows(k)
        id_row = id_rows[k]
        prev_id = id_rows[k - 1][:, SPAN - 1 :] if k else before
        next_id = id_rows[k + 1][:, :1] if k + 1 < ranks else after
        ids = jnp.transpose(jnp.broadcast_to(id_row, (SPAN, SPAN)))
        idcol[k] = ids
        steps = dtg[k]
        cum = lax.dot_general(
            -rate[...] * steps, up, NN, precision=lax.Precision.HIGHEST, preferred_element_type=F32
        )
        cum_t = jnp.transpose(jnp.concatenate([cum, pad], axis=0))
        dt_t = jnp.transpose(jnp.concatenate([steps, pad], axis=0))
        ltok[at, :] = cum_t
        dttok[at, :] = dt_t
        for ch in range(CHUNKS):
            mine = slice(ch * HC, (ch + 1) * HC)
            both = jnp.concatenate([cum[mine], steps[mine]], axis=0)
            lhead[ch, k] = both
            tc[ch, at, :] = jnp.transpose(
                jnp.concatenate([both, jnp.zeros((LANES - 2 * HC, SPAN), F32)], axis=0)
            )
        rest = jnp.exp(cum_t[SPAN - 1 :, :] - cum_t)
        c_in[at, :] = jnp.where(ids == prev_id, jnp.exp(cum_t), 0.0)
        c_out[at, :] = jnp.where(ids == next_id, rest, 0.0)
        c_end[at, :] = jnp.where(ids == id_row[:, SPAN - 1 :], rest, 0.0) * dt_t
        neg[k] = jnp.where(ordered & (ids == id_row), 0.0, -1e30)
        cross[k] = mm(bg[at, :], cg[at, :], NT)

    lane_row = lax.broadcasted_iota(jnp.int32, (LANES, CW), 0)
    lane_col = lax.broadcasted_iota(jnp.int32, (LANES, CW), 1) // P_SIZE

    def spread_of(ch):
        return jnp.where(lane_row == lane_col + ch * HC, 1.0, 0.0).astype(BF)

    def decay_of(k, spread):
        return left2(c_in[k * SPAN + SPAN - 8 : (k + 1) * SPAN, :], spread)[7:, :]

    def summarise(ch):
        for copy in chunk_copies(ch):
            wait_in(copy)
        spread = spread_of(ch)
        for k in range(ranks):
            at = rows(k)
            xs = xg[ch, at, :].astype(F32) * left2(c_end[at, :], spread)
            dyc = dyg[ch, at, :].astype(F32) * left2(c_in[at, :], spread)
            fresh[ch, k] = right2(bg[at, :], xs, TN)
            message[ch, k] = right2(cg[at, :], dyc, TN)

    def s_copy(ch):
        return remote(
            s_out.at[ch], s_in.at[ch], send_z.at[0, ch], recv_z.at[0, ch],
            jnp.minimum(context + ranks, contexts - 1), tensor,
        )

    def a_copy(ch):
        return remote(
            a_out.at[ch], a_in.at[ch], send_z.at[1, ch], recv_z.at[1, ch],
            jnp.maximum(context - ranks, 0), tensor,
        )

    def pass_state(ch):
        @pl.when(plane > 0)
        def _():
            s_copy(ch).wait_recv()

        @pl.when(plane < last)
        def _():
            spread = spread_of(ch)
            state = s_in[ch]
            for k in range(ranks):
                state = decay_of(k, spread) * state + fresh[ch, k]
            s_out[ch] = state
            s_copy(ch).start()

    def pass_adjoint(ch):
        @pl.when(plane < last)
        def _():
            a_copy(ch).wait_recv()

        @pl.when(plane > 0)
        def _():
            spread = spread_of(ch)
            state = a_in[ch]
            for k in range(ranks - 1, -1, -1):
                state = decay_of(k, spread) * state + message[ch, k]
            a_out[ch] = state
            a_copy(ch).start()

    def inside(ch):
        def block(k, carry):
            at = pl.ds(pl.multiple_of(k * SPAN, SPAN), SPAN)
            cross_t = cross[k]
            hide = neg[k]
            total = score[k]
            x_k, dy_k, cols, heads = xg[ch, at, :], dyg[ch, at, :], tc[ch, at, :], lhead[ch, k]
            agrees = []
            for h in range(HC):
                cut = slice(h * P_SIZE, (h + 1) * P_SIZE)
                x_h, dy_h = x_k[:, cut], dy_k[:, cut]
                w = jnp.exp((heads[h : h + 1, :] - cols[:, h : h + 1]) + hide)
                u[ch, at, cut] = left2(w * cross_t, dy_h)
                q = w * mm(x_h, dy_h, NT) * cols[:, HC + h : HC + h + 1]
                total = total + q
                agrees.append(jnp.sum(q * cross_t, axis=0, keepdims=True))
            score[k] = total
            agree[ch, k] = jnp.concatenate(agrees + agrees, axis=0)
            return carry

        lax.fori_loop(0, ranks, block, 0)

    def gi_copies(ch):
        copies = []
        for dr in list(range(1, ranks)) + [0]:
            to = lax.rem(rank + dr, ranks)
            src = gi.at[ch, pl.ds(pl.multiple_of(to * SPAN, SPAN), SPAN), :]
            dst = gi_o.at[:, pl.ds(pl.multiple_of(rank * WIDE + ch * CW, CW), CW)]
            if dr == 0:
                copies.append(pltpu.make_async_copy(src, dst, recv_o.at[ch, 0]))
            else:
                copies.append(
                    remote(src, dst, send_o.at[ch, dr], recv_o.at[ch, dr], base + to, tensor)
                )
        return copies

    def finish(ch):
        spread = spread_of(ch)
        states = [s_in[ch]]
        for k in range(ranks):
            states.append(decay_of(k, spread) * states[k] + fresh[ch, k])
        adj = a_in[ch]
        for k in range(ranks - 1, -1, -1):
            at = rows(k)
            in_e = left2(c_in[at, :], spread)
            out_e = left2(c_out[at, :], spread)
            dt_e = left2(dttok[at, :], spread)
            state = states[k]
            x_f = xg[ch, at, :].astype(F32)
            dyc = dyg[ch, at, :].astype(F32) * in_e
            total_u = u[ch, at, :] + right2(bg[at, :], adj) * out_e
            gi[ch, at, :] = (total_u * dt_e).astype(BF)
            gc[at, :] += both3(dyc, state, NT)
            gb[at, :] += both3(x_f * out_e * dt_e, adj, NT)
            dyy[at, :] += left2(dyc * right2(cg[at, :], state), spread, NT)
            xu[at, :] += left2(x_f * total_u, spread, NT)
            meet = jnp.sum(states[k + 1] * adj, axis=0, keepdims=True)
            meets[k] += left2(jnp.broadcast_to(meet, (8, CW)), spread, NT)
            adj = in_e[SPAN - 1 :, :] * adj + message[ch, k]
        for copy in gi_copies(ch):
            copy.start()

    def step(it, carry):
        @pl.when(it < CHUNKS)
        def _():
            summarise(it)

        ahead = it - plane

        @pl.when((ahead >= 0) & (ahead < CHUNKS))
        def _():
            pass_state(ahead)

        behind = it - (last - plane)

        @pl.when((behind >= 0) & (behind < CHUNKS))
        def _():
            pass_adjoint(behind)

        @pl.when(it < CHUNKS)
        def _():
            inside(it)

        @pl.when(it >= last)
        def _():
            finish(it - last)

        return carry

    lax.fori_loop(0, CHUNKS + last, step, 0)

    rate_row = jnp.transpose(
        jnp.concatenate([jnp.broadcast_to(rate[...], (PER, SPAN)), pad], axis=0)
    )
    for k in range(ranks):
        at = rows(k)
        id_row = id_rows[k]
        next_id = id_rows[k + 1][:, :1] if k + 1 < ranks else after
        ids = idcol[k]
        gb[at, :] += left2(score[k], cg[at, :])
        gc[at, :] += left2(score[k], bg[at, :], TN)
        agree_k = jnp.concatenate([agree[ch, k][:HC] for ch in range(CHUNKS)] + [pad], axis=0)
        slope = jnp.transpose(agree_k) + dyy[at, :] - dttok[at, :] * xu[at, :]
        same = jnp.where((ids == id_row) & ordered, 1.0, 0.0).astype(BF)
        tails = right2(same, slope) + jnp.where(ids == next_id, meets[k][:1], 0.0)
        gs[k] = jnp.transpose(xu[at, :] - rate_row * tails)[:PER, :]

    def map_copies(dr):
        to = lax.rem(rank + dr, ranks)
        there = pl.ds(pl.multiple_of(to * SPAN, SPAN), SPAN)
        at = pl.ds(pl.multiple_of(rank * N, N), N)
        pairs = [
            (gb.at[there, :], gb_o.at[:, at]),
            (gc.at[there, :], gc_o.at[:, at]),
            (gs.at[to], gs_o.at[pl.ds(pl.multiple_of(rank * PER, PER), PER), :]),
        ]
        if dr == 0:
            return [pltpu.make_async_copy(s, d, local.at[n]) for n, (s, d) in enumerate(pairs)]
        return [
            remote(s, d, send_m.at[dr * 3 + n], recv_m.at[dr * 3 + n], base + to, tensor)
            for n, (s, d) in enumerate(pairs)
        ]

    order = list(range(1, ranks)) + [0]
    for dr in order:
        for copy in map_copies(dr):
            copy.start()
    for d in range(1, contexts):
        doc_copy(d).wait_send()
    for dr in order[:-1]:
        for copy in small_copies(dr):
            copy.wait_send()
    for ch in range(CHUNKS):
        for copy in chunk_copies(ch):
            if copy.is_remote:
                copy.wait_send()
        for copy in gi_copies(ch):
            copy.wait()

        @pl.when(plane < last)
        def _():
            s_copy(ch).wait_send()

        @pl.when(plane > 0)
        def _():
            a_copy(ch).wait_send()

    for dr in order:
        for copy in map_copies(dr):
            copy.wait()


def shards(head_inputs, step_sizes, decay_rate, input_map, output_map, document, grad_output):
    heads_here = decay_rate.shape[0]
    ranks = heads_here // PER
    contexts = lax.axis_size("context")
    tensors = lax.axis_size("tensor")
    tokens = ranks * SPAN
    rank = lax.axis_index("context") % ranks
    anywhere = pl.BlockSpec(memory_space=pl.ANY)
    vmem = pl.BlockSpec(memory_space=pltpu.VMEM)
    shape = jax.ShapeDtypeStruct
    mem = pltpu.VMEM
    dma = pltpu.SemaphoreType.DMA
    doc = document.astype(F32)[None, :]
    rate = lax.dynamic_slice(decay_rate, (rank * PER,), (PER,))[:, None]
    return pl.pallas_call(
        functools.partial(mega_kernel, ranks, tensors, contexts),
        out_shape=(
            shape((SPAN, ranks * WIDE), BF),
            shape((heads_here, SPAN), F32),
            shape((SPAN, ranks * N), F32),
            shape((SPAN, ranks * N), F32),
        ),
        in_specs=[anywhere] * 5 + [vmem] * 2,
        out_specs=(anywhere,) * 4,
        scratch_shapes=[
            mem((CHUNKS, tokens, CW), BF),
            mem((CHUNKS, tokens, CW), BF),
            mem((tokens, N), BF),
            mem((tokens, N), BF),
            mem((ranks, PER, SPAN), F32),
            mem((contexts, 1, SPAN), F32),
            mem((CHUNKS, N, CW), F32),
            mem((CHUNKS, N, CW), F32),
            mem((CHUNKS, N, CW), F32),
            mem((CHUNKS, N, CW), F32),
            mem((CHUNKS, ranks, N, CW), F32),
            mem((CHUNKS, ranks, N, CW), F32),
            mem((CHUNKS, tokens, CW), F32),
            mem((CHUNKS, tokens, CW), BF),
            mem((CHUNKS, tokens, LANES), F32),
            mem((tokens, LANES), F32),
            mem((tokens, LANES), F32),
            mem((tokens, LANES), F32),
            mem((tokens, LANES), F32),
            mem((tokens, LANES), F32),
            mem((ranks, SPAN, SPAN), F32),
            mem((CHUNKS, ranks, 2 * HC, SPAN), F32),
            mem((ranks, SPAN, SPAN), F32),
            mem((ranks, SPAN, SPAN), F32),
            mem((ranks, SPAN, SPAN), F32),
            mem((CHUNKS, ranks, 2 * HC, SPAN), F32),
            mem((tokens, LANES), F32),
            mem((tokens, LANES), F32),
            mem((ranks, 8, LANES), F32),
            mem((tokens, N), F32),
            mem((tokens, N), F32),
            mem((ranks, PER, SPAN), F32),
            dma((CHUNKS, ranks)),
            dma((CHUNKS, ranks)),
            dma((CHUNKS, ranks * tensors)),
            dma((CHUNKS, ranks * tensors)),
            dma((ranks * 3,)),
            dma((ranks * 3,)),
            dma((contexts,)),
            dma((contexts,)),
            dma((2, CHUNKS)),
            dma((2, CHUNKS)),
            dma((CHUNKS, ranks)),
            dma((CHUNKS, ranks)),
            dma((ranks * 3,)),
            dma((ranks * 3,)),
            dma((4,)),
        ],
        compiler_params=pltpu.CompilerParams(
            collective_id=0, has_side_effects=True, vmem_limit_bytes=48 * 1024 * 1024
        ),
        name="mixer",
    )(head_inputs, input_map, output_map, step_sizes, grad_output, doc, rate)


def solution(mesh):
    placed = (
        P("context", "tensor"),
        P("tensor", "context"),
        P("tensor"),
        P("context", "tensor"),
        P("context", "tensor"),
        P("context"),
        P(("context", "tensor"), None),
    )
    return jax.shard_map(
        shards,
        mesh=mesh,
        in_specs=placed,
        out_specs=(
            P("context", "tensor"),
            P("tensor", "context"),
            P("context", "tensor"),
            P("context", "tensor"),
        ),
        check_vma=False,
    )
```

time: 583 us -> 71.2 us (0.12)
  waiting for transfers between devices: 199 us -> 0 us
  local copies, waits for them, and re-layouts: 116 us -> 8.61 us
  other arithmetic: 99.4 us -> 0.01 us
  blocking collectives: 82.1 us -> 0 us
  Pallas kernels: 0 us -> 61.6 us
  matrix products: 57.6 us -> 0 us
  between operations: 16.9 us -> 0.68 us
  starting transfers between devices: 10.1 us -> 0 us
    all_gather x2 -> x0, waiting for transfers between devices: 187 us -> none  [entering(): gathered = jax.tree.map(lambda a: lax.all_gather(a, axis), part)]
    add x30 -> x0, other arithmetic: 92.2 us -> none  [the longest x29 91.6 us: link_pairs(): return (earlier[0] * decay_late, spread * earlier[1] + later[1])]
    dynamic_slice x30 -> x0, local copies, waits for them, and re-layouts: 67.3 us -> none  [one(): lax.dynamic_index_in_dim(a, source, 0, False)]
    pallas_call x0 -> x1, Pallas kernels: none -> 61.6 us  [shards(): pl.pallas_call(functools.partial(mega_kernel, ranks, tensors, contexts),...]
    dot_general x13 -> x0, matrix products: 57.6 us -> none  [the longest x1 7.68 us: shards(): jnp.einsum('kjgn,kghnp,ghkj->kjghp', in_f, exit_adjoints, out_coef, preci...]
    all_gather x2 -> x0, blocking collectives: 50.5 us -> none  [entering(): gathered = jax.tree.map(lambda a: lax.all_gather(a, axis), part)]
    unnamed x1 -> x0, blocking collectives: 31.6 us -> none
    another operation x8 -> x0, local copies, waits for them, and re-layouts: 14.3 us -> none
  transfers between devices with their start and end apart: 5 -> 0, of which waited for: 3 -> 0; matrix products, arithmetic and copies ran while one was open for 15% -> 0% of each run, Pallas kernels for 0% -> 0%
where the time goes in v2:
time: 71.2 us; the launch traced here: 70.9 us
  Pallas kernels  61.6 us (87%)
  local copies, waits for them, and re-layouts  8.61 us (12%)
    pallas_call x1, Pallas kernels, shards(): pl.pallas_call(functools.partial(mega_kernel, ranks, tensors, contexts),...  61.6 us
    unnamed x18, local copies, waits for them, and re-layouts  8.46 us

profile of v2, /device:TPU:1, one launch (start us, length us, event | category | flops | bytes accessed | tf_op | source)
XLA Modules:
  0.0 70.9 jit_solution(2803745108191131365)
XLA Ops:
  0.6 0.0 copy-start
  0.6 0.0 copy-start.5
  0.7 0.6 copy-done
  1.3 0.0 copy-start.6
  1.3 0.1 dynamic-slice_bitcast_fusion
  1.4 0.6 copy-done.6
  2.0 0.1 copy.11.rate
  2.0 0.0 copy-done.5
  2.0 0.0 copy-start.1
  2.0 1.2 %copy-done.1 = bf16[128,4096]{1,0:T(8,128)(2,1)S(1)} copy-done((bf16[128,4096]{1,0:T(8,128)(2,1)S(1)}, bf16[128,4096]{1,0:T(8,128)(2,1)}, u32[]{:S(2)}) %copy-start.1) | copy-done | bytes 1048600
  3.3 0.0 copy-start.2
  3.3 1.2 %copy-done.2 = bf16[64,8192]{1,0:T(8,128)(2,1)S(1)} copy-done((bf16[64,8192]{1,0:T(8,128)(2,1)S(1)}, bf16[64,8192]{1,0:T(8,128)(2,1)}, u32[]{:S(2)}) %copy-start.2) | copy-done | bytes 1048600
  4.5 0.0 copy-start.3
  4.5 0.9 %copy-done.3 = bf16[128,512]{1,0:T(8,128)(2,1)S(1)} copy-done((bf16[128,512]{1,0:T(8,128)(2,1)S(1)}, bf16[128,512]{1,0:T(8,128)(2,1)}, u32[]{:S(2)}) %copy-start.3) | copy-done | bytes 131096
  5.4 0.0 copy-start.4
  5.4 0.9 %copy-done.4 = bf16[128,512]{1,0:T(8,128)(2,1)S(1)} copy-done((bf16[128,512]{1,0:T(8,128)(2,1)S(1)}, bf16[128,512]{1,0:T(8,128)(2,1)}, u32[]{:S(2)}) %copy-start.4) | copy-done | bytes 131096
  6.3 61.6 %mixer.1 = (bf16[128,4096]{1,0:T(8,128)(2,1)S(1)}, f32[64,128]{1,0:T(8,128)S(1)}, f32[128,512]{1,0:T(8,128)S(1)}, f32[128,512]{1,0:T(8,128)S(1)}) custom-call(bf16[128,4096]{1,0:T(8,128)(2,1)S(1)} %copy-done.1, bf16[128,512]{1,0:T(8,128)(2,1)S(1)} %copy-done.3, bf16[128,512]{1,0:T(8,128)(2,1)S(1)} %copy-done.4, f32[64,128]{1,0:T(8,128)S(1)} %copy-done.5, ...), custom_call_target="tpu_custom_call" | custom-call | tf_op jit(solution)/shard_map/mixer/pallas_call | solution.py:450
  67.9 1.0 %copy.16 = bf16[128,4096]{1,0:T(8,128)(2,1)} copy(bf16[128,4096]{1,0:T(8,128)(2,1)S(1)} %get-tuple-element.8) | data formatting | bytes 2097152
  68.9 0.6 copy.17
  69.5 0.7 copy.18
  70.2 0.7 copy.19
  (1 shorter events, 0.0 us)
Async XLA Ops:
  0.6 0.7 copy-start
  0.6 1.4 %copy-start.5 = (f32[64,128]{1,0:T(8,128)S(1)}, f32[64,128]{1,0:T(8,128)}, u32[]{:S(2)}) copy-start(f32[64,128]{1,0:T(8,128)} %dt.1) | copy-start | bytes 98308
  1.3 0.7 copy-start.6
  2.0 1.2 %copy-start.1 = (bf16[128,4096]{1,0:T(8,128)(2,1)S(1)}, bf16[128,4096]{1,0:T(8,128)(2,1)}, u32[]{:S(2)}) copy-start(bf16[128,4096]{1,0:T(8,128)(2,1)} %x.1) | copy-start | bytes 3145732
  3.3 1.2 %copy-start.2 = (bf16[64,8192]{1,0:T(8,128)(2,1)S(1)}, bf16[64,8192]{1,0:T(8,128)(2,1)}, u32[]{:S(2)}) copy-start(bf16[64,8192]{1,0:T(8,128)(2,1)} %dy.1) | copy-start | bytes 3145732
  4.5 0.9 %copy-start.3 = (bf16[128,512]{1,0:T(8,128)(2,1)S(1)}, bf16[128,512]{1,0:T(8,128)(2,1)}, u32[]{:S(2)}) copy-start(bf16[128,512]{1,0:T(8,128)(2,1)} %b.1) | copy-start | bytes 393220
  5.4 0.9 %copy-start.4 = (bf16[128,512]{1,0:T(8,128)(2,1)S(1)}, bf16[128,512]{1,0:T(8,128)(2,1)}, u32[]{:S(2)}) copy-start(bf16[128,512]{1,0:T(8,128)(2,1)} %c.1) | copy-start | bytes 393220

commit v3 on v2

--- a/solution.py
+++ b/solution.py
@@ -56,8 +56,8 @@
 
 
 def mega_kernel(
-    ranks, tensors, contexts, x, b, c, dt, dy, doc, rate, gi_o, gs_o, gb_o, gc_o,
-    xg, dyg, bg, cg, dtg, docs, s_in, a_in, s_out, a_out, fresh, message, u, gi,
+    ranks, tensors, contexts, x, b, c, dt, dy, doc, rate_in, gi_o, gs_o, gb_o, gc_o,
+    xg, dyg, bg, cg, dtg, docs, rates, s_in, a_in, s_out, a_out, fresh, message, decays, u, gi,
     tc, ltok, dttok, c_in, c_out, c_end, idcol, lhead, cross, neg, score, agree,
     dyy, xu, meets, gb, gc, gs,
     send_x, recv_x, send_dy, recv_dy, send_s, recv_s, send_doc, recv_doc,
@@ -181,17 +181,24 @@
     up = ordered.astype(F32)
     pad = jnp.zeros((LANES - PER, SPAN), F32)
 
+    heads = rate_in.shape[1]
+    rate_wide = rate_in[...]
+    if heads < LANES:
+        rate_wide = jnp.concatenate([rate_wide, jnp.zeros((1, LANES - heads), F32)], axis=1)
+    rates[...] = jnp.transpose(jnp.broadcast_to(rate_wide, (LANES, LANES)))
+    rate = rates[pl.ds(pl.multiple_of(rank * PER, PER), PER), :]
+
     own_doc.wait()
     for d in range(1, contexts):
         doc_copy(d).wait_recv()
     for dr in list(range(1, ranks)) + [0]:
         for copy in small_copies(dr):
             wait_in(copy)
-    before = docs[jnp.maximum(base - 1, 0)][:, SPAN - 1 :]
+    before = docs[jnp.maximum(base - 1, 0)].astype(F32)[:, SPAN - 1 :]
     before = jnp.where(plane == 0, -1.0, before)
-    after = docs[jnp.minimum(base + ranks, contexts - 1)][:, :1]
+    after = docs[jnp.minimum(base + ranks, contexts - 1)].astype(F32)[:, :1]
     after = jnp.where(plane == last, -1.0, after)
-    id_rows = [docs[base + k] for k in range(ranks)]
+    id_rows = [docs[base + k].astype(F32) for k in range(ranks)]
     for k in range(ranks):
         at = rows(k)
         id_row = id_rows[k]
@@ -201,7 +208,7 @@
         idcol[k] = ids
         steps = dtg[k]
         cum = lax.dot_general(
-            -rate[...] * steps, up, NN, precision=lax.Precision.HIGHEST, preferred_element_type=F32
+            -rate * steps, up, NN, precision=lax.Precision.HIGHEST, preferred_element_type=F32
         )
         cum_t = jnp.transpose(jnp.concatenate([cum, pad], axis=0))
         dt_t = jnp.transpose(jnp.concatenate([steps, pad], axis=0))
@@ -227,9 +234,6 @@
     def spread_of(ch):
         return jnp.where(lane_row == lane_col + ch * HC, 1.0, 0.0).astype(BF)
 
-    def decay_of(k, spread):
-        return left2(c_in[k * SPAN + SPAN - 8 : (k + 1) * SPAN, :], spread)[7:, :]
-
     def summarise(ch):
         for copy in chunk_copies(ch):
             wait_in(copy)
@@ -237,9 +241,22 @@
         for k in range(ranks):
             at = rows(k)
             xs = xg[ch, at, :].astype(F32) * left2(c_end[at, :], spread)
-            dyc = dyg[ch, at, :].astype(F32) * left2(c_in[at, :], spread)
+            in_e = left2(c_in[at, :], spread)
+            dyc = dyg[ch, at, :].astype(F32) * in_e
+            decays[ch, k] = in_e[SPAN - 1 :, :]
             fresh[ch, k] = right2(bg[at, :], xs, TN)
             message[ch, k] = right2(cg[at, :], dyc, TN)
+        state = fresh[ch, 0]
+        decay = decays[ch, 0]
+        for k in range(1, ranks):
+            state = decays[ch, k] * state + fresh[ch, k]
+            decay = decays[ch, k] * decay
+        s_out[ch] = state
+        state = message[ch, ranks - 1]
+        for k in range(ranks - 2, -1, -1):
+            state = decays[ch, k] * state + message[ch, k]
+        a_out[ch] = state
+        decays[ch, ranks] = decay
 
     def s_copy(ch):
         return remote(
@@ -260,11 +277,7 @@
 
         @pl.when(plane < last)
         def _():
-            spread = spread_of(ch)
-            state = s_in[ch]
-            for k in range(ranks):
-                state = decay_of(k, spread) * state + fresh[ch, k]
-            s_out[ch] = state
+            s_out[ch] += decays[ch, ranks] * s_in[ch]
             s_copy(ch).start()
 
     def pass_adjoint(ch):
@@ -274,11 +287,7 @@
 
         @pl.when(plane > 0)
         def _():
-            spread = spread_of(ch)
-            state = a_in[ch]
-            for k in range(ranks - 1, -1, -1):
-                state = decay_of(k, spread) * state + message[ch, k]
-            a_out[ch] = state
+            a_out[ch] += decays[ch, ranks] * a_in[ch]
             a_copy(ch).start()
 
     def inside(ch):
@@ -298,30 +307,50 @@
                 total = total + q
                 agrees.append(jnp.sum(q * cross_t, axis=0, keepdims=True))
             score[k] = total
-            agree[ch, k] = jnp.concatenate(agrees + agrees, axis=0)
+            agree[ch, k] = jnp.concatenate(agrees, axis=0)
             return carry
 
         lax.fori_loop(0, ranks, block, 0)
 
-    def gi_copies(ch):
-        copies = []
-        for dr in list(range(1, ranks)) + [0]:
-            to = lax.rem(rank + dr, ranks)
-            src = gi.at[ch, pl.ds(pl.multiple_of(to * SPAN, SPAN), SPAN), :]
-            dst = gi_o.at[:, pl.ds(pl.multiple_of(rank * WIDE + ch * CW, CW), CW)]
-            if dr == 0:
-                copies.append(pltpu.make_async_copy(src, dst, recv_o.at[ch, 0]))
-            else:
-                copies.append(
-                    remote(src, dst, send_o.at[ch, dr], recv_o.at[ch, dr], base + to, tensor)
-                )
-        return copies
+    def gi_pair(ch, to):
+        return (
+            gi.at[ch, pl.ds(to * SPAN, SPAN), :],
+            gi_o.at[:, pl.ds(pl.multiple_of(rank * WIDE + ch * CW, CW), CW)],
+        )
+
+    def gi_local(ch, to):
+        return pltpu.make_async_copy(*gi_pair(ch, to), recv_o.at[ch, rank])
+
+    def gi_remote(ch, to):
+        return remote(
+            *gi_pair(ch, to), send_o.at[ch, to], recv_o.at[ch, rank], base + to, tensor
+        )
+
+    def gi_start(ch, to):
+        @pl.when(rank == to)
+        def _():
+            gi_local(ch, to).start()
+
+        @pl.when(rank != to)
+        def _():
+            gi_remote(ch, to).start()
+
+    def gi_wait(ch, other):
+        @pl.when(rank == other)
+        def _():
+            gi_local(ch, other).wait()
+
+        @pl.when(rank != other)
+        def _():
+            remote(
+                *gi_pair(ch, other), send_o.at[ch, other], recv_o.at[ch, other], base + other, tensor
+            ).wait()
 
     def finish(ch):
         spread = spread_of(ch)
         states = [s_in[ch]]
         for k in range(ranks):
-            states.append(decay_of(k, spread) * states[k] + fresh[ch, k])
+            states.append(decays[ch, k] * states[k] + fresh[ch, k])
         adj = a_in[ch]
         for k in range(ranks - 1, -1, -1):
             at = rows(k)
@@ -333,16 +362,14 @@
             dyc = dyg[ch, at, :].astype(F32) * in_e
             total_u = u[ch, at, :] + right2(bg[at, :], adj) * out_e
             gi[ch, at, :] = (total_u * dt_e).astype(BF)
+            gi_start(ch, k)
             gc[at, :] += both3(dyc, state, NT)
             gb[at, :] += both3(x_f * out_e * dt_e, adj, NT)
             dyy[at, :] += left2(dyc * right2(cg[at, :], state), spread, NT)
             xu[at, :] += left2(x_f * total_u, spread, NT)
             meet = jnp.sum(states[k + 1] * adj, axis=0, keepdims=True)
             meets[k] += left2(jnp.broadcast_to(meet, (8, CW)), spread, NT)
-            adj = in_e[SPAN - 1 :, :] * adj + message[ch, k]
-        for copy in gi_copies(ch):
-            copy.start()
-
+            adj = decays[ch, k] * adj + message[ch, k]
     def step(it, carry):
         @pl.when(it < CHUNKS)
         def _():
@@ -373,7 +400,7 @@
     lax.fori_loop(0, CHUNKS + last, step, 0)
 
     rate_row = jnp.transpose(
-        jnp.concatenate([jnp.broadcast_to(rate[...], (PER, SPAN)), pad], axis=0)
+        jnp.concatenate([rates[pl.ds(pl.multiple_of(rank * PER, PER), PER), :], pad], axis=0)
     )
     for k in range(ranks):
         at = rows(k)
@@ -382,7 +409,7 @@
         ids = idcol[k]
         gb[at, :] += left2(score[k], cg[at, :])
         gc[at, :] += left2(score[k], bg[at, :], TN)
-        agree_k = jnp.concatenate([agree[ch, k][:HC] for ch in range(CHUNKS)] + [pad], axis=0)
+        agree_k = jnp.concatenate([agree[ch, k] for ch in range(CHUNKS)] + [pad], axis=0)
         slope = jnp.transpose(agree_k) + dyy[at, :] - dttok[at, :] * xu[at, :]
         same = jnp.where((ids == id_row) & ordered, 1.0, 0.0).astype(BF)
         tails = right2(same, slope) + jnp.where(ids == next_id, meets[k][:1], 0.0)
@@ -417,8 +444,8 @@
         for copy in chunk_copies(ch):
             if copy.is_remote:
                 copy.wait_send()
-        for copy in gi_copies(ch):
-            copy.wait()
+        for other in range(ranks):
+            gi_wait(ch, other)
 
         @pl.when(plane < last)
         def _():
@@ -439,14 +466,11 @@
     contexts = lax.axis_size("context")
     tensors = lax.axis_size("tensor")
     tokens = ranks * SPAN
-    rank = lax.axis_index("context") % ranks
-    anywhere = pl.BlockSpec(memory_space=pl.ANY)
+    hbm = pl.BlockSpec(memory_space=pltpu.HBM)
     vmem = pl.BlockSpec(memory_space=pltpu.VMEM)
     shape = jax.ShapeDtypeStruct
     mem = pltpu.VMEM
     dma = pltpu.SemaphoreType.DMA
-    doc = document.astype(F32)[None, :]
-    rate = lax.dynamic_slice(decay_rate, (rank * PER,), (PER,))[:, None]
     return pl.pallas_call(
         functools.partial(mega_kernel, ranks, tensors, contexts),
         out_shape=(
@@ -455,21 +479,23 @@
             shape((SPAN, ranks * N), F32),
             shape((SPAN, ranks * N), F32),
         ),
-        in_specs=[anywhere] * 5 + [vmem] * 2,
-        out_specs=(anywhere,) * 4,
+        in_specs=[hbm] * 5 + [vmem] * 2,
+        out_specs=(hbm,) * 4,
         scratch_shapes=[
             mem((CHUNKS, tokens, CW), BF),
             mem((CHUNKS, tokens, CW), BF),
             mem((tokens, N), BF),
             mem((tokens, N), BF),
             mem((ranks, PER, SPAN), F32),
-            mem((contexts, 1, SPAN), F32),
+            mem((contexts, 1, SPAN), jnp.int32),
+            mem((LANES, LANES), F32),
             mem((CHUNKS, N, CW), F32),
             mem((CHUNKS, N, CW), F32),
             mem((CHUNKS, N, CW), F32),
             mem((CHUNKS, N, CW), F32),
             mem((CHUNKS, ranks, N, CW), F32),
             mem((CHUNKS, ranks, N, CW), F32),
+            mem((CHUNKS, ranks + 1, 1, CW), F32),
             mem((CHUNKS, tokens, CW), F32),
             mem((CHUNKS, tokens, CW), BF),
             mem((CHUNKS, tokens, LANES), F32),
@@ -483,7 +509,7 @@
             mem((ranks, SPAN, SPAN), F32),
             mem((ranks, SPAN, SPAN), F32),
             mem((ranks, SPAN, SPAN), F32),
-            mem((CHUNKS, ranks, 2 * HC, SPAN), F32),
+            mem((CHUNKS, ranks, HC, SPAN), F32),
             mem((tokens, LANES), F32),
             mem((tokens, LANES), F32),
             mem((ranks, 8, LANES), F32),
@@ -507,10 +533,10 @@
             dma((4,)),
         ],
         compiler_params=pltpu.CompilerParams(
-            collective_id=0, has_side_effects=True, vmem_limit_bytes=48 * 1024 * 1024
+            collective_id=0, has_side_effects=True, vmem_limit_bytes=63 * 1024 * 1024
         ),
         name="mixer",
-    )(head_inputs, input_map, output_map, step_sizes, grad_output, doc, rate)
+    )(head_inputs, input_map, output_map, step_sizes, grad_output, document[None, :], decay_rate[None, :])
 
 
 def solution(mesh):

time: 71.2 us -> 66.8 us (0.938)
  local copies, waits for them, and re-layouts: 8.61 us -> 4.7 us
    unnamed x18 -> x10, local copies, waits for them, and re-layouts: 8.46 us -> 4.7 us
where the time goes in v3:
time: 66.8 us; the launch traced here: 66.6 us
  Pallas kernels  61.3 us (92%)
  local copies, waits for them, and re-layouts  4.7 us (7%)
    pallas_call x1, Pallas kernels, shards(): pl.pallas_call(functools.partial(mega_kernel, ranks, tensors, contexts),...  61.3 us
    unnamed x10, local copies, waits for them, and re-layouts  4.7 us

profile of v3, /device:TPU:1, one launch (start us, length us, event | category | flops | bytes accessed | tf_op | source)
XLA Modules:
  0.0 66.6 jit_solution(14445162130496426230)
XLA Ops:
  0.6 61.3 %mixer.1 = (bf16[128,4096]{1,0:T(8,128)(2,1)}, f32[64,128]{1,0:T(8,128)}, f32[128,512]{1,0:T(8,128)}, f32[128,512]{1,0:T(8,128)}) custom-call(bf16[128,4096]{1,0:T(8,128)(2,1)} %x.1, bf16[128,512]{1,0:T(8,128)(2,1)} %b.1, bf16[128,512]{1,0:T(8,128)(2,1)} %c.1, f32[64,128]{1,0:T(8,128)} %dt.1, bf16[64,8192]{1,0:T(8,128)(2,1)} %dy.1, s32[1,128]{1,0:T(1,128)} %bitcast.2, ...), custom_call_target="tpu_custom_call" | custom-call | tf_op jit(solution)/shard_map/mixer/pallas_call | solution.py:474
  61.9 0.0 copy-start.2
  61.9 0.0 copy-start.1
  61.9 2.3 %copy.15 = bf16[128,4096]{1,0:T(8,128)(2,1)} copy(bf16[128,4096]{1,0:T(8,128)(2,1)} %get-tuple-element.8) | data formatting | bytes 2097152
  64.3 0.0 copy-done.2
  64.3 0.6 copy.16
  64.9 0.0 copy-done.1
  64.9 0.0 copy-start
  64.9 0.7 %copy.17 = f32[128,512]{1,0:T(8,128)} copy(f32[128,512]{1,0:T(8,128)S(1)} %copy-done.1) | data formatting | bytes 524288
  65.6 0.3 copy-done
  65.9 0.7 %copy.18 = f32[128,512]{1,0:T(8,128)} copy(f32[128,512]{1,0:T(8,128)S(1)} %copy-done) | data formatting | bytes 524288
Async XLA Ops:
  61.9 2.4 %copy-start.2 = (f32[64,128]{1,0:T(8,128)S(1)}, f32[64,128]{1,0:T(8,128)}, u32[]{:S(2)}) copy-start(f32[64,128]{1,0:T(8,128)} %get-tuple-element.9) | copy-start | bytes 98308
  61.9 3.0 %copy-start.1 = (f32[128,512]{1,0:T(8,128)S(1)}, f32[128,512]{1,0:T(8,128)}, u32[]{:S(2)}) copy-start(f32[128,512]{1,0:T(8,128)} %get-tuple-element.10) | copy-start | bytes 786436
  64.9 1.0 %copy-start = (f32[128,512]{1,0:T(8,128)S(1)}, f32[128,512]{1,0:T(8,128)}, u32[]{:S(2)}) copy-start(f32[128,512]{1,0:T(8,128)} %get-tuple-element.11) | copy-start | bytes 786436

commit v4 on v3

--- a/solution.py
+++ b/solution.py
@@ -57,7 +57,7 @@
 
 def mega_kernel(
     ranks, tensors, contexts, x, b, c, dt, dy, doc, rate_in, gi_o, gs_o, gb_o, gc_o,
-    xg, dyg, bg, cg, dtg, docs, rates, s_in, a_in, s_out, a_out, fresh, message, decays, u, gi,
+    xg, dyg, bg, cg, dtg, docs, rates, s_in, a_in, s_out, a_out, fresh, message, decays, far, u, gi,
     tc, ltok, dttok, c_in, c_out, c_end, idcol, lhead, cross, neg, score, agree,
     dyy, xu, meets, gb, gc, gs,
     send_x, recv_x, send_dy, recv_dy, send_s, recv_s, send_doc, recv_doc,
@@ -65,6 +65,8 @@
 ):
     planes = contexts // ranks
     last = planes - 1
+    short = planes == 4
+    lag = 2 if short else last
     context = lax.axis_index("context")
     tensor = lax.axis_index("tensor")
     rank = lax.rem(context, ranks)
@@ -168,6 +170,16 @@
     def _():
         a_in[...] = jnp.zeros_like(a_in)
 
+    if short:
+
+        @pl.when(plane <= 1)
+        def _():
+            far[0] = jnp.zeros_like(far[0])
+
+        @pl.when(plane >= last - 1)
+        def _():
+            far[1] = jnp.zeros_like(far[1])
+
     score[...] = jnp.zeros_like(score)
     dyy[...] = jnp.zeros_like(dyy)
     xu[...] = jnp.zeros_like(xu)
@@ -270,6 +282,55 @@
             jnp.maximum(context - ranks, 0), tensor,
         )
 
+    def s_far(ch):
+        return remote(
+            far.at[2, ch], far.at[0, ch], send_z.at[2, ch], recv_z.at[2, ch],
+            jnp.minimum(context + ranks, contexts - 1), tensor,
+        )
+
+    def a_far(ch):
+        return remote(
+            far.at[3, ch], far.at[1, ch], send_z.at[3, ch], recv_z.at[3, ch],
+            jnp.maximum(context - ranks, 0), tensor,
+        )
+
+    def pass_first(ch):
+        @pl.when(plane < last)
+        def _():
+            s_copy(ch).start()
+
+        @pl.when(plane > 0)
+        def _():
+            a_copy(ch).start()
+
+    def pass_second(ch):
+        @pl.when(plane > 0)
+        def _():
+            s_copy(ch).wait_recv()
+
+        @pl.when((plane > 0) & (plane < last))
+        def _():
+            far[2, ch] = decays[ch, ranks] * s_in[ch]
+            s_far(ch).start()
+
+        @pl.when(plane < last)
+        def _():
+            a_copy(ch).wait_recv()
+
+        @pl.when((plane > 0) & (plane < last))
+        def _():
+            far[3, ch] = decays[ch, ranks] * a_in[ch]
+            a_far(ch).start()
+
+    def pass_last(ch):
+        @pl.when(plane > 1)
+        def _():
+            s_far(ch).wait_recv()
+
+        @pl.when(plane < last - 1)
+        def _():
+            a_far(ch).wait_recv()
+
     def pass_state(ch):
         @pl.when(plane > 0)
         def _():
@@ -348,10 +409,10 @@
 
     def finish(ch):
         spread = spread_of(ch)
-        states = [s_in[ch]]
+        states = [s_in[ch] + far[0, ch] if short else s_in[ch]]
         for k in range(ranks):
             states.append(decays[ch, k] * states[k] + fresh[ch, k])
-        adj = a_in[ch]
+        adj = a_in[ch] + far[1, ch] if short else a_in[ch]
         for k in range(ranks - 1, -1, -1):
             at = rows(k)
             in_e = left2(c_in[at, :], spread)
@@ -375,29 +436,72 @@
         def _():
             summarise(it)
 
-        ahead = it - plane
-
-        @pl.when((ahead >= 0) & (ahead < CHUNKS))
-        def _():
-            pass_state(ahead)
-
-        behind = it - (last - plane)
-
-        @pl.when((behind >= 0) & (behind < CHUNKS))
-        def _():
-            pass_adjoint(behind)
+        if short:
+
+            @pl.when(it < CHUNKS)
+            def _():
+                pass_first(it)
+
+            @pl.when((it >= 1) & (it <= CHUNKS))
+            def _():
+                pass_second(it - 1)
+
+        else:
+            ahead = it - plane
+
+            @pl.when((ahead >= 0) & (ahead < CHUNKS))
+            def _():
+                pass_state(ahead)
+
+            behind = it - (last - plane)
+
+            @pl.when((behind >= 0) & (behind < CHUNKS))
+            def _():
+                pass_adjoint(behind)
 
         @pl.when(it < CHUNKS)
         def _():
             inside(it)
 
-        @pl.when(it >= last)
-        def _():
-            finish(it - last)
+        @pl.when(it >= lag)
+        def _():
+            if short:
+                pass_last(it - lag)
+            finish(it - lag)
 
         return carry
 
-    lax.fori_loop(0, CHUNKS + last, step, 0)
+    lax.fori_loop(0, CHUNKS + lag, step, 0)
+
+    def map_copies(to, source):
+        there = pl.ds(to * SPAN, SPAN)
+        at = pl.ds(pl.multiple_of(rank * N, N), N)
+        pairs = [
+            (gb.at[there, :], gb_o.at[:, at]),
+            (gc.at[there, :], gc_o.at[:, at]),
+            (gs.at[to], gs_o.at[pl.ds(pl.multiple_of(rank * PER, PER), PER), :]),
+        ]
+        own = [pltpu.make_async_copy(s, d, local.at[n]) for n, (s, d) in enumerate(pairs)]
+        away = [
+            remote(
+                s, d, send_m.at[to * 3 + n], recv_m.at[source * 3 + n], base + to, tensor
+            )
+            for n, (s, d) in enumerate(pairs)
+        ]
+        return own, away
+
+    def map_do(to, source, act):
+        own, away = map_copies(to, source)
+
+        @pl.when(rank == to)
+        def _():
+            for copy in own:
+                act(copy)
+
+        @pl.when(rank != to)
+        def _():
+            for copy in away:
+                act(copy)
 
     rate_row = jnp.transpose(
         jnp.concatenate([rates[pl.ds(pl.multiple_of(rank * PER, PER), PER), :], pad], axis=0)
@@ -414,27 +518,9 @@
         same = jnp.where((ids == id_row) & ordered, 1.0, 0.0).astype(BF)
         tails = right2(same, slope) + jnp.where(ids == next_id, meets[k][:1], 0.0)
         gs[k] = jnp.transpose(xu[at, :] - rate_row * tails)[:PER, :]
-
-    def map_copies(dr):
-        to = lax.rem(rank + dr, ranks)
-        there = pl.ds(pl.multiple_of(to * SPAN, SPAN), SPAN)
-        at = pl.ds(pl.multiple_of(rank * N, N), N)
-        pairs = [
-            (gb.at[there, :], gb_o.at[:, at]),
-            (gc.at[there, :], gc_o.at[:, at]),
-            (gs.at[to], gs_o.at[pl.ds(pl.multiple_of(rank * PER, PER), PER), :]),
-        ]
-        if dr == 0:
-            return [pltpu.make_async_copy(s, d, local.at[n]) for n, (s, d) in enumerate(pairs)]
-        return [
-            remote(s, d, send_m.at[dr * 3 + n], recv_m.at[dr * 3 + n], base + to, tensor)
-            for n, (s, d) in enumerate(pairs)
-        ]
+        map_do(k, rank, lambda copy: copy.start())
 
     order = list(range(1, ranks)) + [0]
-    for dr in order:
-        for copy in map_copies(dr):
-            copy.start()
     for d in range(1, contexts):
         doc_copy(d).wait_send()
     for dr in order[:-1]:
@@ -455,9 +541,15 @@
         def _():
             a_copy(ch).wait_send()
 
-    for dr in order:
-        for copy in map_copies(dr):
-            copy.wait()
+        if short:
+
+            @pl.when((plane > 0) & (plane < last))
+            def _():
+                s_far(ch).wait_send()
+                a_far(ch).wait_send()
+
+    for other in range(ranks):
+        map_do(other, other, lambda copy: copy.wait())
 
 
 def shards(head_inputs, step_sizes, decay_rate, input_map, output_map, document, grad_output):
@@ -496,6 +588,7 @@
             mem((CHUNKS, ranks, N, CW), F32),
             mem((CHUNKS, ranks, N, CW), F32),
             mem((CHUNKS, ranks + 1, 1, CW), F32),
+            mem((4, CHUNKS, N, CW), F32),
             mem((CHUNKS, tokens, CW), F32),
             mem((CHUNKS, tokens, CW), BF),
             mem((CHUNKS, tokens, LANES), F32),
@@ -524,8 +617,8 @@
             dma((ranks * 3,)),
             dma((contexts,)),
             dma((contexts,)),
-            dma((2, CHUNKS)),
-            dma((2, CHUNKS)),
+            dma((4, CHUNKS)),
+            dma((4, CHUNKS)),
             dma((CHUNKS, ranks)),
             dma((CHUNKS, ranks)),
             dma((ranks * 3,)),

time: 66.8 us -> 64.7 us (0.969)
  Pallas kernels: 61.3 us -> 59.1 us
    pallas_call x1, Pallas kernels: 61.3 us -> 59.1 us  [shards(): pl.pallas_call(functools.partial(mega_kernel, ranks, tensors, contexts),...]
where the time goes in v4:
time: 64.7 us; the launch traced here: 64.5 us
  Pallas kernels  59.1 us (91%)
  local copies, waits for them, and re-layouts  4.7 us (7%)
  between operations  0.66 us (1%)
    pallas_call x1, Pallas kernels, shards(): pl.pallas_call(functools.partial(mega_kernel, ranks, tensors, contexts),...  59.1 us
    unnamed x10, local copies, waits for them, and re-layouts  4.7 us

profile of v4, /device:TPU:1, one launch (start us, length us, event | category | flops | bytes accessed | tf_op | source)
XLA Modules:
  0.0 64.5 jit_solution(727234046695250407)
XLA Ops:
  0.6 59.1 %mixer.1 = (bf16[128,4096]{1,0:T(8,128)(2,1)}, f32[64,128]{1,0:T(8,128)}, f32[128,512]{1,0:T(8,128)}, f32[128,512]{1,0:T(8,128)}) custom-call(bf16[128,4096]{1,0:T(8,128)(2,1)} %x.1, bf16[128,512]{1,0:T(8,128)(2,1)} %b.1, bf16[128,512]{1,0:T(8,128)(2,1)} %c.1, f32[64,128]{1,0:T(8,128)} %dt.1, bf16[64,8192]{1,0:T(8,128)(2,1)} %dy.1, s32[1,128]{1,0:T(1,128)} %bitcast.2, ...), custom_call_target="tpu_custom_call" | custom-call | tf_op jit(solution)/shard_map/mixer/pallas_call | solution.py:566
  59.8 0.0 copy-start.2
  59.8 0.0 copy-start.1
  59.8 2.3 %copy.15 = bf16[128,4096]{1,0:T(8,128)(2,1)} copy(bf16[128,4096]{1,0:T(8,128)(2,1)} %get-tuple-element.8) | data formatting | bytes 2097152
  62.1 0.0 copy-done.2
  62.1 0.6 copy.16
  62.7 0.0 copy-done.1
  62.7 0.0 copy-start
  62.7 0.7 %copy.17 = f32[128,512]{1,0:T(8,128)} copy(f32[128,512]{1,0:T(8,128)S(1)} %copy-done.1) | data formatting | bytes 524288
  63.5 0.3 copy-done
  63.8 0.7 %copy.18 = f32[128,512]{1,0:T(8,128)} copy(f32[128,512]{1,0:T(8,128)S(1)} %copy-done) | data formatting | bytes 524288
Async XLA Ops:
  59.8 2.4 %copy-start.2 = (f32[64,128]{1,0:T(8,128)S(1)}, f32[64,128]{1,0:T(8,128)}, u32[]{:S(2)}) copy-start(f32[64,128]{1,0:T(8,128)} %get-tuple-element.9) | copy-start | bytes 98308
  59.8 3.0 %copy-start.1 = (f32[128,512]{1,0:T(8,128)S(1)}, f32[128,512]{1,0:T(8,128)}, u32[]{:S(2)}) copy-start(f32[128,512]{1,0:T(8,128)} %get-tuple-element.10) | copy-start | bytes 786436
  62.7 1.0 %copy-start = (f32[128,512]{1,0:T(8,128)S(1)}, f32[128,512]{1,0:T(8,128)}, u32[]{:S(2)}) copy-start(f32[128,512]{1,0:T(8,128)} %get-tuple-element.11) | copy-start | bytes 786436
